TPU v7x, 32 devices: a whole 2x2x4 slice. The times are simulated.
32 devices in a mesh: ray: 4 (over y, core), cuts: 8 (over z, x).
Axes of the slice: x: 2, y: 2, z: 4, core: 2. Of those that a mesh axis runs over, the one named last changes fastest.
Arguments:
- initial: float32 [16, 16, 4096], P('cuts', 'ray'), may hold values from 0.5 to 1.5
- measured: float32 [4, 32, 16, 4096], P('ray', None, 'cuts'), may hold values from 9.6 to 28.8
- order: int32 [4], replicated, may hold values from 0 to 3, each once
- angle_index: int32 [4, 32], replicated, may hold values from 0 to 2999
Outputs:
- reconstruction: float32 [16, 16, 4096], P('cuts', 'ray')
Inputs may be any that keep to these rules, and one draw needn't show every extreme that they name: Each stored subset appears once; the first 2 entries are the subsets run, in order, and stored subset j is held by index j of ray.
All inputs are finite; a program needn't handle non-finite values.
Results may differ from a plain program's by a relative error of at most 0.0003.
Values sent between devices are 32-bit elements; how exact they have to be, the bound alone decides.
No kernel may reach another device: no remote copies, remote signals or barrier semaphores. Data moves between devices by JAX's collectives and lax.ppermute only.
A program may use at most 64 MiB of HBM per device.

v0:
```python
import jax
import jax.numpy as jnp
from jax import lax
from jax.sharding import PartitionSpec as P

SUBSETS = 2
NANG = 3000
TV_ITERS = 2


TV_STEP = 0.05
TV_EPS = 0.5
angle_group = 2


def broadcast(value, axis, source):
    kept = jnp.where(lax.axis_index(axis) == source, value, 0).astype(value.dtype)
    return lax.psum(kept, axis)


def padded_2(block, sides, width):
    for axis, dim in sides:
        count = lax.axis_size(axis)
        forward = [(i, i + 1) for i in range(count - 1)]
        backward = [(target, source) for source, target in forward]
        low = lax.ppermute(
            lax.slice_in_dim(block, block.shape[dim] - width, None, axis=dim), axis, forward
        )
        high = lax.ppermute(lax.slice_in_dim(block, 0, width, axis=dim), axis, backward)
        block = jnp.concatenate([low, block, high], axis=dim)
    return block


def strip_geometry(angle_row, first_row, total_rows, strip_rows):
    slopes = -1.0 + (2.0 * angle_row.astype(jnp.float32) + 1.0) / NANG
    row_pos = (first_row + jnp.arange(strip_rows, dtype=jnp.int32)).astype(jnp.float32) - (
        total_rows - 1
    ) / 2.0
    spread = slopes[:, None] * row_pos[None, :]
    floor_part = jnp.floor(spread)
    return (floor_part.astype(jnp.int32), spread - floor_part)


def row_windows(padded, starts, width):

    def row_one_row(plane, start):
        return lax.dynamic_slice_in_dim(plane, start, width, 1)

    return jax.vmap(row_one_row, in_axes=(1, 0), out_axes=1)(padded, starts)


def plane_windows(plane, starts, width):

    def plane_one_row(start):
        return lax.dynamic_slice_in_dim(plane, start, width, 1)

    return jax.vmap(plane_one_row, out_axes=1)(starts)


def project_block(padded, shifts, fraction, margin, width):
    angle_count, rows = shifts.shape
    groups = angle_count // angle_group

    def project_one_angle(shift_row, frac_row):
        window = row_windows(padded, margin - shift_row - 1, width + 1)
        weight = frac_row[None, :, None]
        return jnp.sum((1.0 - weight) * window[:, :, 1:] + weight * window[:, :, :-1], axis=1)

    def one_group(pieces):
        return jax.vmap(project_one_angle)(pieces[0], pieces[1])

    result = lax.map(
        one_group,
        (shifts.reshape(groups, angle_group, rows), fraction.reshape(groups, angle_group, rows)),
    )
    return result.reshape(angle_count, padded.shape[0], width)


def back_block(res_padded, shifts, fraction, margin, width):
    angle_count, rows = shifts.shape
    groups = angle_count // angle_group
    slices = res_padded.shape[1]

    def back_one_angle(plane, shift_row, frac_row):
        window = plane_windows(plane, margin + shift_row, width + 1)
        weight = frac_row[None, :, None]
        return (1.0 - weight) * window[:, :, :-1] + weight * window[:, :, 1:]

    def add_group(summed, pieces):
        terms = jax.vmap(back_one_angle)(pieces[0], pieces[1], pieces[2])
        return (summed + jnp.sum(terms, axis=0), None)

    planes = res_padded.reshape((groups, angle_group) + res_padded.shape[1:])
    summed, _ = lax.scan(
        add_group,
        jnp.zeros((slices, rows, width), jnp.float32),
        (
            planes,
            shifts.reshape(groups, angle_group, rows),
            fraction.reshape(groups, angle_group, rows),
        ),
    )
    return summed


def tv_step(extended, first_row, first_slice, total_rows, total_slices):
    count_s, count_r, breadth = extended.shape
    row_ids = first_row + jnp.arange(count_r, dtype=jnp.int32)
    slice_ids = first_slice + jnp.arange(count_s, dtype=jnp.int32)
    row_in = (row_ids >= 0) & (row_ids < total_rows)
    slice_in = (slice_ids >= 0) & (slice_ids < total_slices)
    centre = extended[:-1, :-1]
    cell_in = slice_in[:-1, None] & row_in[None, :-1]
    valid_r = cell_in & row_in[None, 1:]
    valid_s = cell_in & slice_in[1:, None]
    step_r = jnp.where(valid_r[:, :, None], extended[:-1, 1:] - centre, 0.0)
    step_s = jnp.where(valid_s[:, :, None], extended[1:, :-1] - centre, 0.0)
    along_c = jnp.concatenate(
        [centre[:, :, 1:] - centre[:, :, :-1], jnp.zeros_like(centre[:, :, :1])], axis=2
    )
    step_c = jnp.where(cell_in[:, :, None], along_c, 0.0)
    magnitude = jnp.sqrt(step_s * step_s + step_r * step_r + step_c * step_c + TV_EPS * TV_EPS)
    flow_r = step_r / magnitude
    flow_s = step_s / magnitude
    flow_c = step_c / magnitude
    inner_c = flow_c[1:, 1:]
    spread = flow_r[1:, 1:] - flow_r[1:, :-1] + flow_s[1:, 1:] - flow_s[:-1, 1:]
    spread = spread + inner_c - jnp.pad(inner_c[:, :, :-1], ((0, 0), (0, 0), (1, 0)))
    return extended[1:-1, 1:-1] + TV_STEP * spread


def on_device(initial, measured, order, angle_index):
    slices, strip_rows, breadth = initial.shape
    ray_count = lax.axis_size("ray")
    cut_count = lax.axis_size("cuts")
    ray_place = lax.axis_index("ray")
    cut_place = lax.axis_index("cuts")
    total_rows = strip_rows * ray_count
    total_slices = slices * cut_count
    angle_total = angle_index.shape[1]
    margin = total_rows // 2 + 2
    stored = measured[0]
    current = initial
    for subset in range(SUBSETS):
        subset_slot = order[subset]
        shifts, fraction = strip_geometry(
            angle_index[subset_slot], ray_place * strip_rows, total_rows, strip_rows
        )
        padded = jnp.pad(current, ((0, 0), (0, 0), (margin, margin)))
        partial_value = project_block(padded, shifts, fraction, margin, breadth)
        totals = lax.psum(partial_value, "ray")
        residual = broadcast(stored - totals, "ray", subset_slot)
        res_padded = jnp.pad(residual, ((0, 0), (0, 0), (margin, margin)))
        current = current + back_block(res_padded, shifts, fraction, margin, breadth) / (
            total_rows * angle_total
        )
        for tv_turn in range(TV_ITERS):
            extended = padded_2(current, (("ray", 1), ("cuts", 0)), 1)
            current = tv_step(
                extended,
                ray_place * strip_rows - 1,
                cut_place * slices - 1,
                total_rows,
                total_slices,
            )
    return current


def solution(mesh):
    return jax.shard_map(
        on_device,
        mesh=mesh,
        in_specs=(P("cuts", "ray", None), P("ray", None, "cuts", None), P(), P()),
        out_specs=P("cuts", "ray", None),
        check_vma=False,
    )
```

profile of v0, /device:TPU:1, one launch (start us, length us, event | category | flops | bytes accessed | tf_op | source)
XLA Modules:
  0.0 1349.5 jit_solution(12900914432349245809)
XLA Ops:
  14.4 270.8 %while.65 = (s32[]{:T(128)}, f32[16,2,2,4096]{3,2,1,0:T(2,128)S(1)}, f32[16,2,4]{2,1,0:T(2,128)S(1)}, f32[2,4,4116]{2,0,1:T(2,128)S(1)}, s32[16,2,4]{2,1,0:T(2,128)S(1)}, /*index=5*/s32[]{:T(128)}, s32[]{:T(128)}, s32[]{:T(128)}) while((s32[]{:T(128)}, f32[16,2,2,4096]{3,2,1,0:T(2,128)S(1)}, f32[16,2,4]{2,1,0:T(2,128)S(1)}, ...), condition=%wide.region_2.3_spmd, body=%wide.region_0.2_spmd.sunk | while | flops 245828 | bytes 789350 | solution.py:72
  287.0 37.4 %all-reduce.21.cloned.1.call-done = f32[32,2,4096]{2,1,0:T(2,128)} async-done(((f32[32,2,4096]{2,1,0:T(2,128)}), f32[32,2,4096]{2,1,0:T(2,128)}) %all-reduce.21.cloned.1.call-update) | async-done | bytes 1048592 | tf_op jit(solution)/shard_map/psum | solution.py:151
  327.6 36.7 %all-reduce.23.cloned.1.call-done = f32[32,2,4096]{2,1,0:T(2,128)} async-done(((f32[32,2,4096]{2,1,0:T(2,128)}), f32[32,2,4096]{2,1,0:T(2,128)}) %all-reduce.23.cloned.1.call-update) | async-done | bytes 1048592 | tf_op jit(solution)/shard_map/psum | solution.py:18
  366.7 274.4 %while.69 = (s32[]{:T(128)}, f32[2,4,4096]{2,0,1:T(2,128)S(1)}, f32[16,2,4]{2,1,0:T(2,128)S(1)}, f32[16,2,2,4116]{3,2,1,0:T(2,128)S(1)}, s32[16,2,4]{2,1,0:T(2,128)S(1)}, /*index=5*/s32[]{:T(128)}, s32[]{:T(128)}, s32[]{:T(128)}) while((s32[]{:T(128)}, f32[2,4,4096]{2,0,1:T(2,128)S(1)}, f32[16,2,4]{2,1,0:T(2,128)S(1)}, ...), condition=%wide.region_7.8_spmd.clone, body=%wide.region_5.7_spmd.clone.sunk | while | flops 294981 | bytes 1248752 | solution.py:94
  366.8 16.3 %while.74 = (s32[]{:T(128)}, f32[2,2,4116]{2,1,0:T(2,128)S(1)}, s32[8,3]{0,1:T(4,128)S(1)}, f32[8,2,4097]{2,1,0:T(2,128)S(1)}, s32[]{:T(128)}) while((s32[]{:T(128)}, f32[2,2,4116]{2,1,0:T(2,128)S(1)}, s32[8,3]{0,1:T(4,128)S(1)}, f32[8,2,4097]{2,1,0:T(2,128)S(1)}, s32[]{:T(128)}) %tuple.230), condition=%wide.while_cond.1, body=%wide.while_body.1.sunk | while | flops 2 | bytes 67701 | solution.py:55
  384.0 16.3 %while.74 = (s32[]{:T(128)}, f32[2,2,4116]{2,1,0:T(2,128)S(1)}, s32[8,3]{0,1:T(4,128)S(1)}, f32[8,2,4097]{2,1,0:T(2,128)S(1)}, s32[]{:T(128)}) while((s32[]{:T(128)}, f32[2,2,4116]{2,1,0:T(2,128)S(1)}, s32[8,3]{0,1:T(4,128)S(1)}, f32[8,2,4097]{2,1,0:T(2,128)S(1)}, s32[]{:T(128)}) %tuple.230), condition=%wide.while_cond.1, body=%wide.while_body.1.sunk | while | flops 2 | bytes 67701 | solution.py:55
  401.1 16.3 %while.74 = (s32[]{:T(128)}, f32[2,2,4116]{2,1,0:T(2,128)S(1)}, s32[8,3]{0,1:T(4,128)S(1)}, f32[8,2,4097]{2,1,0:T(2,128)S(1)}, s32[]{:T(128)}) while((s32[]{:T(128)}, f32[2,2,4116]{2,1,0:T(2,128)S(1)}, s32[8,3]{0,1:T(4,128)S(1)}, f32[8,2,4097]{2,1,0:T(2,128)S(1)}, s32[]{:T(128)}) %tuple.230), condition=%wide.while_cond.1, body=%wide.while_body.1.sunk | while | flops 2 | bytes 67701 | solution.py:55
  435.4 16.3 %while.74 = (s32[]{:T(128)}, f32[2,2,4116]{2,1,0:T(2,128)S(1)}, s32[8,3]{0,1:T(4,128)S(1)}, f32[8,2,4097]{2,1,0:T(2,128)S(1)}, s32[]{:T(128)}) while((s32[]{:T(128)}, f32[2,2,4116]{2,1,0:T(2,128)S(1)}, s32[8,3]{0,1:T(4,128)S(1)}, f32[8,2,4097]{2,1,0:T(2,128)S(1)}, s32[]{:T(128)}) %tuple.230), condition=%wide.while_cond.1, body=%wide.while_body.1.sunk | while | flops 2 | bytes 67701 | solution.py:55
  452.6 16.3 %while.74 = (s32[]{:T(128)}, f32[2,2,4116]{2,1,0:T(2,128)S(1)}, s32[8,3]{0,1:T(4,128)S(1)}, f32[8,2,4097]{2,1,0:T(2,128)S(1)}, s32[]{:T(128)}) while((s32[]{:T(128)}, f32[2,2,4116]{2,1,0:T(2,128)S(1)}, s32[8,3]{0,1:T(4,128)S(1)}, f32[8,2,4097]{2,1,0:T(2,128)S(1)}, s32[]{:T(128)}) %tuple.230), condition=%wide.while_cond.1, body=%wide.while_body.1.sunk | while | flops 2 | bytes 67701 | solution.py:55
  469.7 16.3 %while.74 = (s32[]{:T(128)}, f32[2,2,4116]{2,1,0:T(2,128)S(1)}, s32[8,3]{0,1:T(4,128)S(1)}, f32[8,2,4097]{2,1,0:T(2,128)S(1)}, s32[]{:T(128)}) while((s32[]{:T(128)}, f32[2,2,4116]{2,1,0:T(2,128)S(1)}, s32[8,3]{0,1:T(4,128)S(1)}, f32[8,2,4097]{2,1,0:T(2,128)S(1)}, s32[]{:T(128)}) %tuple.230), condition=%wide.while_cond.1, body=%wide.while_body.1.sunk | while | flops 2 | bytes 67701 | solution.py:55
  504.0 16.3 %while.74 = (s32[]{:T(128)}, f32[2,2,4116]{2,1,0:T(2,128)S(1)}, s32[8,3]{0,1:T(4,128)S(1)}, f32[8,2,4097]{2,1,0:T(2,128)S(1)}, s32[]{:T(128)}) while((s32[]{:T(128)}, f32[2,2,4116]{2,1,0:T(2,128)S(1)}, s32[8,3]{0,1:T(4,128)S(1)}, f32[8,2,4097]{2,1,0:T(2,128)S(1)}, s32[]{:T(128)}) %tuple.230), condition=%wide.while_cond.1, body=%wide.while_body.1.sunk | while | flops 2 | bytes 67701 | solution.py:55
  521.2 16.3 %while.74 = (s32[]{:T(128)}, f32[2,2,4116]{2,1,0:T(2,128)S(1)}, s32[8,3]{0,1:T(4,128)S(1)}, f32[8,2,4097]{2,1,0:T(2,128)S(1)}, s32[]{:T(128)}) while((s32[]{:T(128)}, f32[2,2,4116]{2,1,0:T(2,128)S(1)}, s32[8,3]{0,1:T(4,128)S(1)}, f32[8,2,4097]{2,1,0:T(2,128)S(1)}, s32[]{:T(128)}) %tuple.230), condition=%wide.while_cond.1, body=%wide.while_body.1.sunk | while | flops 2 | bytes 67701 | solution.py:55
  538.3 16.3 %while.74 = (s32[]{:T(128)}, f32[2,2,4116]{2,1,0:T(2,128)S(1)}, s32[8,3]{0,1:T(4,128)S(1)}, f32[8,2,4097]{2,1,0:T(2,128)S(1)}, s32[]{:T(128)}) while((s32[]{:T(128)}, f32[2,2,4116]{2,1,0:T(2,128)S(1)}, s32[8,3]{0,1:T(4,128)S(1)}, f32[8,2,4097]{2,1,0:T(2,128)S(1)}, s32[]{:T(128)}) %tuple.230), condition=%wide.while_cond.1, body=%wide.while_body.1.sunk | while | flops 2 | bytes 67701 | solution.py:55
  572.6 16.3 %while.74 = (s32[]{:T(128)}, f32[2,2,4116]{2,1,0:T(2,128)S(1)}, s32[8,3]{0,1:T(4,128)S(1)}, f32[8,2,4097]{2,1,0:T(2,128)S(1)}, s32[]{:T(128)}) while((s32[]{:T(128)}, f32[2,2,4116]{2,1,0:T(2,128)S(1)}, s32[8,3]{0,1:T(4,128)S(1)}, f32[8,2,4097]{2,1,0:T(2,128)S(1)}, s32[]{:T(128)}) %tuple.230), condition=%wide.while_cond.1, body=%wide.while_body.1.sunk | while | flops 2 | bytes 67701 | solution.py:55
  589.8 16.3 %while.74 = (s32[]{:T(128)}, f32[2,2,4116]{2,1,0:T(2,128)S(1)}, s32[8,3]{0,1:T(4,128)S(1)}, f32[8,2,4097]{2,1,0:T(2,128)S(1)}, s32[]{:T(128)}) while((s32[]{:T(128)}, f32[2,2,4116]{2,1,0:T(2,128)S(1)}, s32[8,3]{0,1:T(4,128)S(1)}, f32[8,2,4097]{2,1,0:T(2,128)S(1)}, s32[]{:T(128)}) %tuple.230), condition=%wide.while_cond.1, body=%wide.while_body.1.sunk | while | flops 2 | bytes 67701 | solution.py:55
  606.9 16.3 %while.74 = (s32[]{:T(128)}, f32[2,2,4116]{2,1,0:T(2,128)S(1)}, s32[8,3]{0,1:T(4,128)S(1)}, f32[8,2,4097]{2,1,0:T(2,128)S(1)}, s32[]{:T(128)}) while((s32[]{:T(128)}, f32[2,2,4116]{2,1,0:T(2,128)S(1)}, s32[8,3]{0,1:T(4,128)S(1)}, f32[8,2,4097]{2,1,0:T(2,128)S(1)}, s32[]{:T(128)}) %tuple.230), condition=%wide.while_cond.1, body=%wide.while_body.1.sunk | while | flops 2 | bytes 67701 | solution.py:55
  624.0 16.3 %while.74 = (s32[]{:T(128)}, f32[2,2,4116]{2,1,0:T(2,128)S(1)}, s32[8,3]{0,1:T(4,128)S(1)}, f32[8,2,4097]{2,1,0:T(2,128)S(1)}, s32[]{:T(128)}) while((s32[]{:T(128)}, f32[2,2,4116]{2,1,0:T(2,128)S(1)}, s32[8,3]{0,1:T(4,128)S(1)}, f32[8,2,4097]{2,1,0:T(2,128)S(1)}, s32[]{:T(128)}) %tuple.230), condition=%wide.while_cond.1, body=%wide.while_body.1.sunk | while | flops 2 | bytes 67701 | solution.py:55
  680.0 270.8 %while.67 = (s32[]{:T(128)}, f32[16,2,2,4096]{3,2,1,0:T(2,128)S(1)}, f32[16,2,4]{2,1,0:T(2,128)S(1)}, f32[2,4,4116]{2,0,1:T(2,128)S(1)}, s32[16,2,4]{2,1,0:T(2,128)S(1)}, /*index=5*/s32[]{:T(128)}, s32[]{:T(128)}, s32[]{:T(128)}) while((s32[]{:T(128)}, f32[16,2,2,4096]{3,2,1,0:T(2,128)S(1)}, f32[16,2,4]{2,1,0:T(2,128)S(1)}, ...), condition=%wide.region_10.11_spmd, body=%wide.region_8.10_spmd.sunk | while | flops 245828 | bytes 789350 | solution.py:72
  952.5 35.1 %all-reduce.25.cloned.1.call-done = f32[32,2,4096]{2,1,0:T(2,128)} async-done(((f32[32,2,4096]{2,1,0:T(2,128)}), f32[32,2,4096]{2,1,0:T(2,128)}) %all-reduce.25.cloned.1.call-update) | async-done | bytes 1048592 | tf_op jit(solution)/shard_map/psum | solution.py:151
  990.5 36.9 %all-reduce.27.cloned.1.call-done = f32[32,2,4096]{2,1,0:T(2,128)} async-done(((f32[32,2,4096]{2,1,0:T(2,128)}), f32[32,2,4096]{2,1,0:T(2,128)}) %all-reduce.27.cloned.1.call-update) | async-done | bytes 1048592 | tf_op jit(solution)/shard_map/psum | solution.py:18
  1029.8 274.4 %while.71 = (s32[]{:T(128)}, f32[2,4,4096]{2,0,1:T(2,128)S(1)}, f32[16,2,4]{2,1,0:T(2,128)S(1)}, f32[16,2,2,4116]{3,2,1,0:T(2,128)S(1)}, s32[16,2,4]{2,1,0:T(2,128)S(1)}, /*index=5*/s32[]{:T(128)}, s32[]{:T(128)}, s32[]{:T(128)}) while((s32[]{:T(128)}, f32[2,4,4096]{2,0,1:T(2,128)S(1)}, f32[16,2,4]{2,1,0:T(2,128)S(1)}, ...), condition=%wide.region_15.16_spmd.clone, body=%wide.region_13.15_spmd.clone.sunk | while | flops 294981 | bytes 1248752 | solution.py:94
  1030.0 16.3 %while.75 = (s32[]{:T(128)}, f32[2,2,4116]{2,1,0:T(2,128)S(1)}, s32[8,3]{0,1:T(4,128)S(1)}, f32[8,2,4097]{2,1,0:T(2,128)S(1)}, s32[]{:T(128)}) while((s32[]{:T(128)}, f32[2,2,4116]{2,1,0:T(2,128)S(1)}, s32[8,3]{0,1:T(4,128)S(1)}, f32[8,2,4097]{2,1,0:T(2,128)S(1)}, s32[]{:T(128)}) %tuple.227), condition=%wide.while_cond.3, body=%wide.while_body.3.sunk | while | flops 2 | bytes 67701 | solution.py:55
  1047.1 16.3 %while.75 = (s32[]{:T(128)}, f32[2,2,4116]{2,1,0:T(2,128)S(1)}, s32[8,3]{0,1:T(4,128)S(1)}, f32[8,2,4097]{2,1,0:T(2,128)S(1)}, s32[]{:T(128)}) while((s32[]{:T(128)}, f32[2,2,4116]{2,1,0:T(2,128)S(1)}, s32[8,3]{0,1:T(4,128)S(1)}, f32[8,2,4097]{2,1,0:T(2,128)S(1)}, s32[]{:T(128)}) %tuple.227), condition=%wide.while_cond.3, body=%wide.while_body.3.sunk | while | flops 2 | bytes 67701 | solution.py:55
  1064.3 16.3 %while.75 = (s32[]{:T(128)}, f32[2,2,4116]{2,1,0:T(2,128)S(1)}, s32[8,3]{0,1:T(4,128)S(1)}, f32[8,2,4097]{2,1,0:T(2,128)S(1)}, s32[]{:T(128)}) while((s32[]{:T(128)}, f32[2,2,4116]{2,1,0:T(2,128)S(1)}, s32[8,3]{0,1:T(4,128)S(1)}, f32[8,2,4097]{2,1,0:T(2,128)S(1)}, s32[]{:T(128)}) %tuple.227), condition=%wide.while_cond.3, body=%wide.while_body.3.sunk | while | flops 2 | bytes 67701 | solution.py:55
  1098.6 16.3 %while.75 = (s32[]{:T(128)}, f32[2,2,4116]{2,1,0:T(2,128)S(1)}, s32[8,3]{0,1:T(4,128)S(1)}, f32[8,2,4097]{2,1,0:T(2,128)S(1)}, s32[]{:T(128)}) while((s32[]{:T(128)}, f32[2,2,4116]{2,1,0:T(2,128)S(1)}, s32[8,3]{0,1:T(4,128)S(1)}, f32[8,2,4097]{2,1,0:T(2,128)S(1)}, s32[]{:T(128)}) %tuple.227), condition=%wide.while_cond.3, body=%wide.while_body.3.sunk | while | flops 2 | bytes 67701 | solution.py:55
  1115.7 16.3 %while.75 = (s32[]{:T(128)}, f32[2,2,4116]{2,1,0:T(2,128)S(1)}, s32[8,3]{0,1:T(4,128)S(1)}, f32[8,2,4097]{2,1,0:T(2,128)S(1)}, s32[]{:T(128)}) while((s32[]{:T(128)}, f32[2,2,4116]{2,1,0:T(2,128)S(1)}, s32[8,3]{0,1:T(4,128)S(1)}, f32[8,2,4097]{2,1,0:T(2,128)S(1)}, s32[]{:T(128)}) %tuple.227), condition=%wide.while_cond.3, body=%wide.while_body.3.sunk | while | flops 2 | bytes 67701 | solution.py:55
  1132.9 16.3 %while.75 = (s32[]{:T(128)}, f32[2,2,4116]{2,1,0:T(2,128)S(1)}, s32[8,3]{0,1:T(4,128)S(1)}, f32[8,2,4097]{2,1,0:T(2,128)S(1)}, s32[]{:T(128)}) while((s32[]{:T(128)}, f32[2,2,4116]{2,1,0:T(2,128)S(1)}, s32[8,3]{0,1:T(4,128)S(1)}, f32[8,2,4097]{2,1,0:T(2,128)S(1)}, s32[]{:T(128)}) %tuple.227), condition=%wide.while_cond.3, body=%wide.while_body.3.sunk | while | flops 2 | bytes 67701 | solution.py:55
  1150.0 16.3 %while.75 = (s32[]{:T(128)}, f32[2,2,4116]{2,1,0:T(2,128)S(1)}, s32[8,3]{0,1:T(4,128)S(1)}, f32[8,2,4097]{2,1,0:T(2,128)S(1)}, s32[]{:T(128)}) while((s32[]{:T(128)}, f32[2,2,4116]{2,1,0:T(2,128)S(1)}, s32[8,3]{0,1:T(4,128)S(1)}, f32[8,2,4097]{2,1,0:T(2,128)S(1)}, s32[]{:T(128)}) %tuple.227), condition=%wide.while_cond.3, body=%wide.while_body.3.sunk | while | flops 2 | bytes 67701 | solution.py:55
  1167.2 16.3 %while.75 = (s32[]{:T(128)}, f32[2,2,4116]{2,1,0:T(2,128)S(1)}, s32[8,3]{0,1:T(4,128)S(1)}, f32[8,2,4097]{2,1,0:T(2,128)S(1)}, s32[]{:T(128)}) while((s32[]{:T(128)}, f32[2,2,4116]{2,1,0:T(2,128)S(1)}, s32[8,3]{0,1:T(4,128)S(1)}, f32[8,2,4097]{2,1,0:T(2,128)S(1)}, s32[]{:T(128)}) %tuple.227), condition=%wide.while_cond.3, body=%wide.while_body.3.sunk | while | flops 2 | bytes 67701 | solution.py:55
  1184.3 16.3 %while.75 = (s32[]{:T(128)}, f32[2,2,4116]{2,1,0:T(2,128)S(1)}, s32[8,3]{0,1:T(4,128)S(1)}, f32[8,2,4097]{2,1,0:T(2,128)S(1)}, s32[]{:T(128)}) while((s32[]{:T(128)}, f32[2,2,4116]{2,1,0:T(2,128)S(1)}, s32[8,3]{0,1:T(4,128)S(1)}, f32[8,2,4097]{2,1,0:T(2,128)S(1)}, s32[]{:T(128)}) %tuple.227), condition=%wide.while_cond.3, body=%wide.while_body.3.sunk | while | flops 2 | bytes 67701 | solution.py:55
  1201.5 16.3 %while.75 = (s32[]{:T(128)}, f32[2,2,4116]{2,1,0:T(2,128)S(1)}, s32[8,3]{0,1:T(4,128)S(1)}, f32[8,2,4097]{2,1,0:T(2,128)S(1)}, s32[]{:T(128)}) while((s32[]{:T(128)}, f32[2,2,4116]{2,1,0:T(2,128)S(1)}, s32[8,3]{0,1:T(4,128)S(1)}, f32[8,2,4097]{2,1,0:T(2,128)S(1)}, s32[]{:T(128)}) %tuple.227), condition=%wide.while_cond.3, body=%wide.while_body.3.sunk | while | flops 2 | bytes 67701 | solution.py:55
  1218.6 16.3 %while.75 = (s32[]{:T(128)}, f32[2,2,4116]{2,1,0:T(2,128)S(1)}, s32[8,3]{0,1:T(4,128)S(1)}, f32[8,2,4097]{2,1,0:T(2,128)S(1)}, s32[]{:T(128)}) while((s32[]{:T(128)}, f32[2,2,4116]{2,1,0:T(2,128)S(1)}, s32[8,3]{0,1:T(4,128)S(1)}, f32[8,2,4097]{2,1,0:T(2,128)S(1)}, s32[]{:T(128)}) %tuple.227), condition=%wide.while_cond.3, body=%wide.while_body.3.sunk | while | flops 2 | bytes 67701 | solution.py:55
  (2230 shorter events, 1822.6 us)
Async XLA Ops:
  6.5 317.9 %all-reduce.21.cloned.1.call-start = ((), (), s32[]{:S(2)}) async-start(), calls=%async_computation | async-start | bytes 2097152 | tf_op jit(solution)/shard_map/psum | solution.py:151
  285.3 1.0 copy-start.1
  285.3 39.1 %copy-start = (f32[1,32,2,4096]{3,2,1,0:T(2,128)S(1)}, f32[1,32,2,4096]{3,2,1,0:T(2,128)}, u32[]{:S(2)}) copy-start(f32[1,32,2,4096]{3,2,1,0:T(2,128)} %param.13) | copy-start | bytes 3145732
  286.3 78.0 %all-reduce.23.cloned.1.call-start = ((), (), s32[]{:S(2)}) async-start(), calls=%async_computation.1 | async-start | bytes 2097152 | tf_op jit(solution)/shard_map/psum | solution.py:18
  327.4 660.2 %all-reduce.25.cloned.1.call-start = ((), (), s32[]{:S(2)}) async-start(), calls=%async_computation.2 | async-start | bytes 2097152 | tf_op jit(solution)/shard_map/psum | solution.py:151
  366.7 274.4 %copy-start.3 = (f32[2,4,4096]{2,1,0:T(4,128)S(1)}, f32[2,4,4096]{2,1,0:T(4,128)}, u32[]{:S(2)}) copy-start(f32[2,4,4096]{2,1,0:T(4,128)} %param.12) | copy-start | bytes 393220
  641.2 5.6 collective-permute-start
  644.8 5.2 collective-permute-start.1
  650.2 5.0 collective-permute-start.2
  653.3 5.7 collective-permute-start.3
  659.9 5.3 collective-permute-start.4
  663.3 5.2 collective-permute-start.5
  668.6 5.9 collective-permute-start.6
  672.6 5.7 collective-permute-start.7
  950.9 1.0 copy-start.2
  951.9 75.6 %all-reduce.27.cloned.1.call-start = ((), (), s32[]{:S(2)}) async-start(), calls=%async_computation.3 | async-start | bytes 2097152 | tf_op jit(solution)/shard_map/psum | solution.py:18
  1304.4 5.5 collective-permute-start.8
  1307.9 5.2 collective-permute-start.9
  1313.3 5.0 collective-permute-start.10
  1316.4 5.7 collective-permute-start.11
  1323.1 5.3 collective-permute-start.12
  1326.4 5.2 collective-permute-start.13
  1331.7 5.9 collective-permute-start.14
  1335.8 5.7 collective-permute-start.15
Sparse Core Ops, SparseCore 0:
  286.4 37.9 all-reduce.20
  327.5 36.7 all-reduce.22
  952.0 35.5 all-reduce.24
  990.6 36.7 all-reduce.26
where the time goes:
time: 1360 us; the launch traced here: 1350 us
  local copies, waits for them, and re-layouts  1050 us (77%)
  waiting for transfers between devices  176 us (13%)
  other arithmetic  47.8 us (4%)
  starting transfers between devices  41 us (3%)
  between operations  18.7 us (1%)
  loops' own time  14.7 us (1%)
    gather x1536, local copies, waits for them, and re-layouts  1030 us
    psum x2, waiting for transfers between devices, broadcast(): return lax.psum(kept, axis)  73.6 us
    psum x2, waiting for transfers between devices, on_device(): totals = lax.psum(partial_value, 'ray')  72.5 us
    ppermute x8, starting transfers between devices, padded_2(): lax.ppermute(lax.slice_in_dim(block, block.shape[dim] - width, None, axis...  28 us
    ppermute x8, waiting for transfers between devices, padded_2(): lax.ppermute(lax.slice_in_dim(block, 0, width, axis=dim), axis, backward)  27.3 us
  transfers between devices with their start and end apart: 20, of which 16 were waited for; matrix products, arithmetic and copies ran while one was open for 0% of the time, Pallas kernels for 0%

commit v1 on v0

v1 whole, which is shorter than its diff:
```python
import functools

import jax
import jax.numpy as jnp
from jax import lax
from jax.experimental import pallas as pl
from jax.experimental.pallas import tpu as pltpu
from jax.sharding import PartitionSpec as P

SUBSETS = 2
NANG = 3000
TV_ITERS = 2
TV_STEP = 0.05
TV_EPS = 0.5
LANES = 128


class Sizes:
    def __init__(self, initial, measured, ray, cuts):
        self.slices, self.strip, self.breadth = initial.shape
        self.angles = measured.shape[1]
        self.ray, self.cuts = ray, cuts
        self.rows = self.strip * ray
        self.total_slices = self.slices * cuts
        self.half = (self.rows + 1) // 2
        self.taps = 2 * self.half + 1
        reach = SUBSETS * (2 * self.half + TV_ITERS)
        self.halo_tiles = -(-2 * reach // LANES)
        self.side = self.halo_tiles * (LANES // 2)
        self.cols = self.breadth // ray
        self.local = self.cols + self.halo_tiles * LANES
        self.image = self.slices * self.rows
        self.sino = self.angles * self.slices


def column_of(z, place, shape):
    lane = lax.broadcasted_iota(jnp.int32, shape, len(shape) - 1)
    return place * z.cols + jnp.where(lane < z.cols + z.side, lane, lane - z.local)


def window(z, ref, lead, target):
    base = target * z.cols
    parts = [ref[lead + (pl.ds(pl.multiple_of(base, LANES), z.cols),)]]
    last = z.breadth - LANES
    for j in range(z.halo_tiles):
        right = base + z.cols + j * LANES
        left = base + (j - z.halo_tiles) * LANES
        at_right = pl.multiple_of(jnp.minimum(right, last), LANES)
        at_left = pl.multiple_of(jnp.maximum(left, 0), LANES)
        tile_r = jnp.where(right <= last, ref[lead + (pl.ds(at_right, LANES),)], 0.0)
        tile_l = jnp.where(left >= 0, ref[lead + (pl.ds(at_left, LANES),)], 0.0)
        lane = j * LANES + lax.broadcasted_iota(jnp.int32, tile_r.shape, tile_r.ndim - 1)
        parts.append(jnp.where(lane < z.side, tile_r, tile_l))
    return jnp.concatenate(parts, axis=-1)


def pack_kernel(z, ref, *outs):
    place = lax.axis_index("ray")
    for step, out in enumerate(outs):
        target = lax.rem(place + step, z.ray)
        out[...] = window(z, ref, (slice(None),) * (len(ref.shape) - 1), target)


def split(value):
    high = value.astype(jnp.bfloat16)
    return high, (value - high.astype(jnp.float32)).astype(jnp.bfloat16)


def tap_weights(z, slope, row, offset):
    spread = slope * (row.astype(jnp.float32) - (z.rows - 1) / 2.0)
    floor_part = jnp.floor(spread)
    frac = spread - floor_part
    near = -floor_part.astype(jnp.int32)
    return jnp.where(offset == near, 1.0 - frac, 0.0) + jnp.where(offset == near - 1, frac, 0.0)


def project(z, x, slope_col):
    group = max(1, 256 // z.image)
    total = jnp.zeros((z.sino, z.local), jnp.float32)
    for first in range(0, z.taps, group):
        count = min(group, z.taps - first)
        shape = (z.sino, count * z.image)
        lane = lax.broadcasted_iota(jnp.int32, shape, 1)
        row = lax.rem(lane, z.rows)
        s_in = lax.rem(lane // z.rows, z.slices)
        offset = first - z.half + lane // z.image
        s_out = lax.rem(lax.broadcasted_iota(jnp.int32, shape, 0), z.slices)
        weight = jnp.where(s_in == s_out, tap_weights(z, slope_col, row, offset), 0.0)
        w_high, w_low = split(weight)
        rolled = [
            pltpu.roll(x, (z.half - first - k) % z.local, 1) if first + k != z.half else x
            for k in range(count)
        ]
        x_high, x_low = split(jnp.concatenate(rolled, axis=0))
        dot = functools.partial(jnp.dot, preferred_element_type=jnp.float32)
        total = total + (dot(w_high, x_high) + dot(w_high, x_low) + dot(w_low, x_high))
    return total


def back(z, residual, slope_row, taps_ref):
    r_high, r_low = split(residual)
    stacked = jnp.concatenate([r_high, r_low, r_high], axis=0)
    shape = (z.taps * z.image, 3 * z.sino)
    line = lax.broadcasted_iota(jnp.int32, shape, 0)
    row = lax.rem(line, z.rows)
    s_out = lax.rem(line // z.rows, z.slices)
    offset = line // z.image - z.half
    lane = lax.broadcasted_iota(jnp.int32, shape, 1)
    weight = jnp.where(
        lax.rem(lane, z.slices) == s_out, tap_weights(z, slope_row, row, offset), 0.0
    )
    w_high, w_low = split(weight)
    weights = jnp.where(lane < 2 * z.sino, w_high, w_low)
    taps_ref[...] = jnp.dot(weights, stacked, preferred_element_type=jnp.float32)
    total = taps_ref[z.half * z.image : (z.half + 1) * z.image, :]
    for k in range(z.taps):
        if k != z.half:
            term = taps_ref[k * z.image : (k + 1) * z.image, :]
            total = total + pltpu.roll(term, (k - z.half) % z.local, 1)
    return total


def tv_steps(z, slabs, place, first_slice):
    shape = slabs[0].shape
    column = column_of(z, place, shape)
    inside = (column >= 0) & (column < z.breadth)
    open_c = inside & (column < z.breadth - 1)
    open_r = lax.broadcasted_iota(jnp.int32, shape, 0) < z.rows - 1
    for _ in range(TV_ITERS):
        flows = []
        for k in range(len(slabs) - 1):
            here = slabs[k]
            ident = first_slice + k
            open_s = (ident >= 0) & (ident < z.total_slices - 1)
            step_s = jnp.where(open_s, slabs[k + 1] - here, 0.0)
            step_r = jnp.where(open_r, pltpu.roll(here, z.rows - 1, 0) - here, 0.0)
            step_c = jnp.where(open_c, pltpu.roll(here, z.local - 1, 1) - here, 0.0)
            scale = lax.rsqrt(
                step_s * step_s + step_r * step_r + step_c * step_c + TV_EPS * TV_EPS
            )
            flows.append((step_s * scale, step_r * scale, step_c * scale))
        done = []
        for k in range(1, len(slabs) - 1):
            flow_s, flow_r, flow_c = flows[k]
            spread = flow_s - flows[k - 1][0]
            spread = spread + flow_r - pltpu.roll(flow_r, 1, 0)
            spread = spread + flow_c - pltpu.roll(flow_c, 1, 1)
            done.append(jnp.where(inside, slabs[k] + TV_STEP * spread, 0.0))
        slabs = done
        first_slice = first_slice + 1
    return slabs


def first_forward_kernel(z, slope_col, *refs):
    pieces, (x_out, f_out, strips) = refs[: z.ray], refs[z.ray :]
    place = lax.axis_index("ray")
    for step, piece in enumerate(pieces):
        strips[lax.rem(place - step + z.ray, z.ray)] = piece[...]
    for s in range(z.slices):
        for r in range(z.ray):
            first = s * z.rows + r * z.strip
            x_out[first : first + z.strip, :] = strips[r, s]
    f_out[...] = project(z, x_out[...], slope_col[...])


def residual_back(z, slot, stored, forward, x, slope_row, scratch):
    taps_ref, kept, sem = scratch
    place = lax.axis_index("ray")
    distance = lax.rem(place - slot + z.ray, z.ray)
    for step, piece in enumerate(stored):

        @pl.when(distance == step)
        def _():
            copy = pltpu.make_async_copy(piece, kept, sem)
            copy.start()
            copy.wait()

    column = column_of(z, place, (z.sino, z.local))
    inside = (column >= 0) & (column < z.breadth)
    residual = jnp.where(inside, kept[...] - forward, 0.0)
    return x + back(z, residual, slope_row, taps_ref) * (1.0 / (z.rows * z.angles))


def first_back_kernel(z, slots, slope_row, x, f, *refs):
    stored, out, scratch = refs[: z.ray], refs[z.ray], refs[z.ray + 1 :]
    out[...] = residual_back(z, slots[0], stored, f[...], x[...], slope_row[...], scratch)


def read_slabs(z, own, low, high):
    blocks = []
    for ref in (low, own, high):
        blocks += [ref[s * z.rows : (s + 1) * z.rows, :] for s in range(ref.shape[0] // z.rows)]
    return blocks


def tv_all(z, own, low, high):
    first = lax.axis_index("cuts") * z.slices - TV_ITERS
    return tv_steps(z, read_slabs(z, own, low, high), lax.axis_index("ray"), first)


def middle_kernel(z, subset, slots, slope_col, slope_row, own, low, high, *refs):
    stored, out, scratch = refs[: z.ray], refs[z.ray], refs[z.ray + 1 :]
    x = jnp.concatenate(tv_all(z, own, low, high), axis=0)
    forward = project(z, x, slope_col[...])
    out[...] = residual_back(z, slots[subset], stored, forward, x, slope_row[...], scratch)


def last_kernel(z, own, low, high, *refs):
    outs, scratch = refs[: z.ray], refs[z.ray]
    for s, slab in enumerate(tv_all(z, own, low, high)):
        for r in range(z.ray):
            scratch[r, s] = slab[r * z.strip : (r + 1) * z.strip, : z.cols]
    place = lax.axis_index("ray")
    for step, out in enumerate(outs):
        out[...] = scratch[lax.rem(place + step, z.ray)]


def join_kernel(z, *refs):
    pieces, out = refs[: z.ray], refs[z.ray]
    place = lax.axis_index("ray")
    for step, piece in enumerate(pieces):
        source = lax.rem(place - step + z.ray, z.ray)
        out[:, :, pl.ds(pl.multiple_of(source * z.cols, LANES), z.cols)] = piece[...]


def call(kernel, name, outs, operands, kinds, scratch=()):
    space = {"v": pltpu.VMEM, "s": pltpu.SMEM, "a": pl.ANY}
    single = isinstance(outs[0], int)
    shapes = [outs] if single else list(outs)
    result = pl.pallas_call(
        kernel,
        name=name,
        out_shape=[jax.ShapeDtypeStruct(s, jnp.float32) for s in shapes],
        in_specs=[pl.BlockSpec(memory_space=space[k]) for k in kinds],
        out_specs=[pl.BlockSpec(memory_space=pltpu.VMEM) for _ in shapes],
        scratch_shapes=list(scratch),
    )(*operands)
    return result[0] if single else result


def spread_over_ray(z, pieces):
    got = [pieces[0]]
    for step in range(1, z.ray):
        pairs = [(i, (i + step) % z.ray) for i in range(z.ray)]
        got.append(lax.ppermute(pieces[step], "ray", pairs))
    return got


def neighbours(z, x):
    width = TV_ITERS * z.rows
    up = [(i, i + 1) for i in range(z.cuts - 1)]
    down = [(i + 1, i) for i in range(z.cuts - 1)]
    low = lax.ppermute(x[x.shape[0] - width :], "cuts", up)
    high = lax.ppermute(x[:width], "cuts", down)
    return low, high


def on_device(ray, cuts, initial, measured, order, angle_index):
    z = Sizes(initial, measured, ray, cuts)
    bind = lambda kernel, *more: functools.partial(kernel, z, *more)
    strips = call(
        bind(pack_kernel), "pack_x", [(z.slices, z.strip, z.local)] * ray, [initial], "v"
    )
    strips = spread_over_ray(z, strips)
    lines = measured.reshape(z.sino, z.breadth)
    stored = call(bind(pack_kernel), "pack_m", [(z.sino, z.local)] * ray, [lines], "v")
    stored = spread_over_ray(z, stored)

    slots = order[:SUBSETS]
    slopes = -1.0 + (2.0 * angle_index[slots].astype(jnp.float32) + 1.0) / NANG
    slopes = jnp.repeat(slopes, z.slices, axis=1)
    slope_col = slopes[:, :, None]
    slope_row = jnp.tile(slopes, (1, 3))[:, None, :]

    whole = (z.image, z.local)
    scratch = [
        pltpu.VMEM((z.taps * z.image, z.local), jnp.float32),
        pltpu.VMEM((z.sino, z.local), jnp.float32),
        pltpu.SemaphoreType.DMA,
    ]
    x, forward = call(
        bind(first_forward_kernel),
        "forward_0",
        [whole, (z.sino, z.local)],
        [slope_col[0], *strips],
        "v" * (1 + ray),
        [pltpu.VMEM((ray, z.slices, z.strip, z.local), jnp.float32)],
    )
    x = call(
        bind(first_back_kernel),
        "back_0",
        whole,
        [slots, slope_row[0], x, forward, *stored],
        "svvv" + "a" * ray,
        scratch,
    )
    for subset in range(1, SUBSETS):
        low, high = neighbours(z, x)
        x = call(
            bind(middle_kernel, subset),
            f"middle_{subset}",
            whole,
            [slots, slope_col[subset], slope_row[subset], x, low, high, *stored],
            "svvvvv" + "a" * ray,
            scratch,
        )
    low, high = neighbours(z, x)
    pieces = call(
        bind(last_kernel),
        "last",
        [(z.slices, z.strip, z.cols)] * ray,
        [x, low, high],
        "vvv",
        [pltpu.VMEM((ray, z.slices, z.strip, z.cols), jnp.float32)],
    )
    pieces = spread_over_ray(z, pieces)
    return call(
        bind(join_kernel), "join", (z.slices, z.strip, z.breadth), pieces, "v" * ray
    )


def solution(mesh):
    return jax.shard_map(
        functools.partial(on_device, mesh.shape["ray"], mesh.shape["cuts"]),
        mesh=mesh,
        in_specs=(P("cuts", "ray", None), P("ray", None, "cuts", None), P(), P()),
        out_specs=P("cuts", "ray", None),
        check_vma=False,
    )
```

time: 1360 us -> 73 us (0.05)
  local copies, waits for them, and re-layouts: 1050 us -> 9.96 us
  waiting for transfers between devices: 176 us -> 23.2 us
  other arithmetic: 47.8 us -> 0.52 us
  starting transfers between devices: 41 us -> 19 us
  Pallas kernels: 0 us -> 18.9 us
  between operations: 18.7 us -> 0.18 us
  loops' own time: 14.7 us -> 0 us
    gather x1600 -> x1, local copies, waits for them, and re-layouts: 1040 us -> 0.56 us  [on_device(): slopes = -1.0 + (2.0 * angle_index[slots].astype(jnp.float32) + 1.0) / NANG]
    psum x4 -> x0, waiting for transfers between devices: 146 us -> none  [the longest x2 73.6 us: broadcast(): return lax.psum(kept, axis)]
    reduce_sum x64 -> x0, other arithmetic: 28.6 us -> none  [the longest x32 15.1 us: add_group(): return (summed + jnp.sum(terms, axis=0), None)]
    ppermute x16 -> x13, starting transfers between devices: 40.8 us -> 19 us  [the longest x9 9.23 us: spread_over_ray(): got.append(lax.ppermute(pieces[step], 'ray', pairs))]
    pallas_call x0 -> x7, Pallas kernels: none -> 18.9 us  [call(): pl.pallas_call(kernel, name=name, out_shape=[jax.ShapeDtypeStruct(s, jnp....]
    another operation x68 -> x0, loops' own time: 14.7 us -> none  [the longest x32 5.17 us: plane_one_row(): return lax.dynamic_slice_in_dim(plane, start, width, 1)]
    ppermute x16 -> x13, waiting for transfers between devices: 29.7 us -> 23.2 us  [the longest x9 14.1 us: spread_over_ray(): got.append(lax.ppermute(pieces[step], 'ray', pairs))]
  transfers between devices with their start and end apart: 20 -> 13, of which waited for: 16 -> 8; matrix products, arithmetic and copies ran while one was open for 0% -> 10% of each run, Pallas kernels for 0% -> 7%
where the time goes in v1:
time: 73 us; the launch traced here: 71.8 us
  waiting for transfers between devices  23.2 us (32%)
  starting transfers between devices  19 us (26%)
  Pallas kernels  18.9 us (26%)
  local copies, waits for them, and re-layouts  9.96 us (14%)
    pallas_call x7, Pallas kernels, call(): pl.pallas_call(kernel, name=name, out_shape=[jax.ShapeDtypeStruct(s, jnp....  18.9 us
    ppermute x9, waiting for transfers between devices, spread_over_ray(): got.append(lax.ppermute(pieces[step], 'ray', pairs))  14.1 us
    ppermute x9, starting transfers between devices, spread_over_ray(): got.append(lax.ppermute(pieces[step], 'ray', pairs))  9.23 us
    ppermute x2, waiting for transfers between devices, neighbours(): high = lax.ppermute(x[:width], 'cuts', down)  7.7 us
    ppermute x2, starting transfers between devices, neighbours(): low = lax.ppermute(x[x.shape[0] - width:], 'cuts', up)  7.2 us
    unnamed x32, local copies, waits for them, and re-layouts  3.47 us
    reshape x1, local copies, waits for them, and re-layouts, on_device(): lines = measured.reshape(z.sino, z.breadth)  2.93 us
    ppermute x2, starting transfers between devices, neighbours(): high = lax.ppermute(x[:width], 'cuts', down)  2.58 us
  transfers between devices with their start and end apart: 13, of which 8 were waited for; matrix products, arithmetic and copies ran while one was open for 10% of the time, Pallas kernels for 7%

profile of v1, /device:TPU:1, one launch (start us, length us, event | category | flops | bytes accessed | tf_op | source)
XLA Modules:
  0.0 71.8 jit_solution(8350731868776399468)
XLA Ops:
  0.0 1.6 %pack_x.1 = (f32[2,4,1152]{2,1,0:T(4,128)}, f32[2,4,1152]{2,1,0:T(4,128)}, f32[2,4,1152]{2,1,0:T(4,128)}, f32[2,4,1152]{2,1,0:T(4,128)}) custom-call(f32[2,4,4096]{2,1,0:T(4,128)} %ref.1), custom_call_target="tpu_custom_call" | custom-call | tf_op jit(solution)/shard_map/pack_x/pallas_call | solution.py:230
  1.6 2.6 %collective-permute-start = (f32[2,4,1152]{2,1,0:T(4,128)}, f32[2,4,1152]{2,1,0:T(4,128)S(1)}, u32[]{:S(2)}, u32[]{:S(2)}) collective-permute-start(f32[2,4,1152]{2,1,0:T(4,128)} %get-tuple-element.20), channel_id=1, source_target_pairs={{0,8},{8,16},{16,24},{24,0},{1,9},{9,17},{17,25},{25,1},{2,10},{10... | collective-permute-start | bytes 110600 | tf_op jit(solution)/shard_map/ppermute | solution.py:245
  4.2 2.9 %reshape.38.ref = f32[64,4096]{1,0:T(8,128)} reshape(f32[1,32,2,4096]{3,2,1,0:T(2,128)} %param.5) | data formatting | bytes 2097152 | tf_op jit(solution)/shard_map/reshape | solution.py:265
  7.1 2.4 %pack_m.1 = (f32[64,1152]{1,0:T(8,128)}, f32[64,1152]{1,0:T(8,128)}, f32[64,1152]{1,0:T(8,128)}, f32[64,1152]{1,0:T(8,128)}) custom-call(f32[64,4096]{1,0:T(8,128)} %reshape.38.ref), custom_call_target="tpu_custom_call" | custom-call | tf_op jit(solution)/shard_map/pack_m/pallas_call | solution.py:230
  9.5 1.7 %collective-permute-start.4 = (f32[64,1152]{1,0:T(8,128)}, f32[64,1152]{1,0:T(8,128)S(1)}, u32[]{:S(2)}, u32[]{:S(2)}) collective-permute-start(f32[64,1152]{1,0:T(8,128)} %get-tuple-element.27), channel_id=1, source_target_pairs={{0,16},{8,24},{16,0},{24,8},{1,17},{9,25},{17,1},{25,9},{2,18},{10... | collective-permute-start | bytes 884744 | tf_op jit(solution)/shard_map/ppermute | solution.py:245
  12.3 0.6 gather_fusion
  13.0 0.7 broadcast_in_dim.24.slope_col
  13.8 0.6 tile.14.slope_row
  14.5 11.0 %collective-permute-done.2.refs_3_ = f32[2,4,1152]{2,1,0:T(4,128)S(1)} collective-permute-done((f32[2,4,1152]{2,1,0:T(4,128)S(1)}, f32[2,4,1152]{2,1,0:T(4,128)S(1)}, u32[]{:S(2)}, u32[]{:S(2)}) %collective-permute-start.2) | collective-permute-done | bytes 36896 | tf_op jit(solution)/shard_map/ppermute | solution.py:245
  25.4 0.6 copy-done.10
  26.0 2.8 %forward_0.1 = (f32[32,1152]{1,0:T(8,128)}, f32[64,1152]{1,0:T(8,128)}) custom-call(f32[64,1]{1,0:T(8,128)} %broadcast_in_dim.24.slope_col, f32[2,4,1152]{2,1,0:T(4,128)} %get-tuple-element.19.refs_0_, f32[2,4,1152]{2,1,0:T(4,128)} %copy-done.8, f32[2,4,1152]{2,1,0:T(4,128)} %copy-done.9, f32[2,4,1152]{2,1,0:T(4,128)} %copy-done.10), custom_call_target="tpu_custom_call" | custom-call | tf_op jit(solution)/shard_map/forward_0/pallas_call | solution.py:230
  28.8 0.7 copy-done.1
  29.7 3.9 %back_0.1.own = f32[32,1152]{1,0:T(8,128)} custom-call(s32[2]{0:T(128)} %get-tuple-element.36.slots, f32[1,192]{1,0:T(1,128)} %tile.14.slope_row, f32[32,1152]{1,0:T(8,128)} %get-tuple-element.23.x, f32[64,1152]{1,0:T(8,128)} %get-tuple-element.24.f, f32[64,1152]{1,0:T(8,128)} %get-tuple-element.25.refs_0_, f32[64,1152]{1,0:T(8,128)} %copy-done.1, ...), custom_call_target="tpu_custom_call" | custom-call | tf_op jit(solution)/shard_map/back_0/pallas_call | solution.py:230
  33.6 3.1 %collective-permute-start.6 = (f32[32,1152]{1,0:T(8,128)}, f32[32,1152]{1,0:T(8,128)S(1)}, u32[]{:S(2)}, u32[]{:S(2)}) collective-permute-start(f32[32,1152]{1,0:T(8,128)} %back_0.1.own), channel_id=1, source_target_pairs={{0,1},{1,2},{2,3},{3,4},{4,5},{5,6},{6,7},{8,9},{9,10},{10,11},{11... | collective-permute-start | bytes 442376 | tf_op jit(solution)/shard_map/ppermute | solution.py:253
  36.8 1.3 %collective-permute-start.7 = (f32[32,1152]{1,0:T(8,128)}, f32[32,1152]{1,0:T(8,128)S(1)}, u32[]{:S(2)}, u32[]{:S(2)}) collective-permute-start(f32[32,1152]{1,0:T(8,128)} %back_0.1.own), channel_id=1, source_target_pairs={{1,0},{2,1},{3,2},{4,3},{5,4},{6,5},{7,6},{9,8},{10,9},{11,10},{12... | collective-permute-start | bytes 442376 | tf_op jit(solution)/shard_map/ppermute | solution.py:254
  38.1 0.7 broadcast_in_dim.23.slope_col
  38.9 0.6 tile.12.slope_row
  39.9 4.0 %collective-permute-done.7.high = f32[32,1152]{1,0:T(8,128)S(1)} collective-permute-done((f32[32,1152]{1,0:T(8,128)}, f32[32,1152]{1,0:T(8,128)S(1)}, u32[]{:S(2)}, u32[]{:S(2)}) %collective-permute-start.7) | collective-permute-done | bytes 147488 | tf_op jit(solution)/shard_map/ppermute | solution.py:254
  43.9 0.7 copy-done.7
  44.6 4.6 %middle_1.1.own = f32[32,1152]{1,0:T(8,128)} custom-call(s32[2]{0:T(128)} %get-tuple-element.36.slots, f32[64,1]{1,0:T(8,128)} %broadcast_in_dim.23.slope_col, f32[1,192]{1,0:T(1,128)} %tile.12.slope_row, f32[32,1152]{1,0:T(8,128)} %back_0.1.own, f32[32,1152]{1,0:T(8,128)} %copy-done.6, f32[32,1152]{1,0:T(8,128)} %copy-done.7, ...), custom_call_target="tpu_custom_call" | custom-call | tf_op jit(solution)/shard_map/middle_1/pallas_call | solution.py:230
  49.2 4.1 %collective-permute-start.8 = (f32[32,1152]{1,0:T(8,128)}, f32[32,1152]{1,0:T(8,128)S(1)}, u32[]{:S(2)}, u32[]{:S(2)}) collective-permute-start(f32[32,1152]{1,0:T(8,128)} %middle_1.1.own), channel_id=1, source_target_pairs={{0,1},{1,2},{2,3},{3,4},{4,5},{5,6},{6,7},{8,9},{9,10},{10,11},{11... | collective-permute-start | bytes 442376 | tf_op jit(solution)/shard_map/ppermute | solution.py:253
  53.3 1.3 %collective-permute-start.9 = (f32[32,1152]{1,0:T(8,128)}, f32[32,1152]{1,0:T(8,128)S(1)}, u32[]{:S(2)}, u32[]{:S(2)}) collective-permute-start(f32[32,1152]{1,0:T(8,128)} %middle_1.1.own), channel_id=1, source_target_pairs={{1,0},{2,1},{3,2},{4,3},{5,4},{6,5},{7,6},{9,8},{10,9},{11,10},{12... | collective-permute-start | bytes 442376 | tf_op jit(solution)/shard_map/ppermute | solution.py:254
  54.6 1.1 %collective-permute-done.8.low = f32[32,1152]{1,0:T(8,128)S(1)} collective-permute-done((f32[32,1152]{1,0:T(8,128)}, f32[32,1152]{1,0:T(8,128)S(1)}, u32[]{:S(2)}, u32[]{:S(2)}) %collective-permute-start.8) | collective-permute-done | bytes 147488 | tf_op jit(solution)/shard_map/ppermute | solution.py:253
  55.7 3.7 %collective-permute-done.9.high = f32[32,1152]{1,0:T(8,128)S(1)} collective-permute-done((f32[32,1152]{1,0:T(8,128)}, f32[32,1152]{1,0:T(8,128)S(1)}, u32[]{:S(2)}, u32[]{:S(2)}) %collective-permute-start.9) | collective-permute-done | bytes 147488 | tf_op jit(solution)/shard_map/ppermute | solution.py:254
  59.4 0.7 copy-done.5
  60.0 2.3 %last.1 = (f32[2,4,1024]{2,1,0:T(4,128)}, f32[2,4,1024]{2,1,0:T(4,128)}, f32[2,4,1024]{2,1,0:T(4,128)}, f32[2,4,1024]{2,1,0:T(4,128)}) custom-call(f32[32,1152]{1,0:T(8,128)} %middle_1.1.own, f32[32,1152]{1,0:T(8,128)} %copy-done.4, f32[32,1152]{1,0:T(8,128)} %copy-done.5), custom_call_target="tpu_custom_call" | custom-call | tf_op jit(solution)/shard_map/last/pallas_call | solution.py:230
  62.3 3.9 %collective-permute-start.10 = (f32[2,4,1024]{2,1,0:T(4,128)}, f32[2,4,1024]{2,1,0:T(4,128)S(1)}, u32[]{:S(2)}, u32[]{:S(2)}) collective-permute-start(f32[2,4,1024]{2,1,0:T(4,128)} %get-tuple-element.30), channel_id=1, source_target_pairs={{0,8},{8,16},{16,24},{24,0},{1,9},{9,17},{17,25},{25,1},{2,10},{10... | collective-permute-start | bytes 98312 | tf_op jit(solution)/shard_map/ppermute | solution.py:245
  66.6 0.9 %collective-permute-done.10.refs_1_ = f32[2,4,1024]{2,1,0:T(4,128)S(1)} collective-permute-done((f32[2,4,1024]{2,1,0:T(4,128)}, f32[2,4,1024]{2,1,0:T(4,128)S(1)}, u32[]{:S(2)}, u32[]{:S(2)}) %collective-permute-start.10) | collective-permute-done | bytes 32800 | tf_op jit(solution)/shard_map/ppermute | solution.py:245
  67.5 1.6 %collective-permute-done.11.refs_2_ = f32[2,4,1024]{2,1,0:T(4,128)S(1)} collective-permute-done((f32[2,4,1024]{2,1,0:T(4,128)}, f32[2,4,1024]{2,1,0:T(4,128)S(1)}, u32[]{:S(2)}, u32[]{:S(2)}) %collective-permute-start.11) | collective-permute-done | bytes 32800 | tf_op jit(solution)/shard_map/ppermute | solution.py:245
  69.2 0.6 collective-permute-done.12.refs_3_
  69.8 0.6 copy-done.13
  70.4 1.5 %join.1 = f32[2,4,4096]{2,1,0:T(4,128)} custom-call(f32[2,4,1024]{2,1,0:T(4,128)} %get-tuple-element.29.refs_0_, f32[2,4,1024]{2,1,0:T(4,128)} %copy-done.11, f32[2,4,1024]{2,1,0:T(4,128)} %copy-done.12, f32[2,4,1024]{2,1,0:T(4,128)} %copy-done.13), custom_call_target="tpu_custom_call" | custom-call | tf_op jit(solution)/shard_map/join/pallas_call | solution.py:230
  (49 shorter events, 2.5 us)
Async XLA Ops:
  0.0 12.3 %copy-start = (s32[4,32]{1,0:T(4,128)S(1)}, s32[4,32]{1,0:T(4,128)}, u32[]{:S(2)}) copy-start(s32[4,32]{1,0:T(4,128)} %param.7) | copy-start | bytes 1540
  1.6 11.3 %collective-permute-start = (f32[2,4,1152]{2,1,0:T(4,128)}, f32[2,4,1152]{2,1,0:T(4,128)S(1)}, u32[]{:S(2)}, u32[]{:S(2)}) collective-permute-start(f32[2,4,1152]{2,1,0:T(4,128)} %get-tuple-element.20), channel_id=1, source_target_pairs={{0,8},{8,16},{16,24},{24,0},{1,9},{9,17},{17,25},{25,1},{2,10},{10... | collective-permute-start | bytes 110600 | tf_op jit(solution)/shard_map/ppermute | solution.py:245
  4.2 10.3 %collective-permute-start.1 = (f32[2,4,1152]{2,1,0:T(4,128)}, f32[2,4,1152]{2,1,0:T(4,128)S(1)}, u32[]{:S(2)}, u32[]{:S(2)}) collective-permute-start(f32[2,4,1152]{2,1,0:T(4,128)} %get-tuple-element.21), channel_id=1, source_target_pairs={{0,16},{8,24},{16,0},{24,8},{1,17},{9,25},{17,1},{25,9},{2,18},{10... | collective-permute-start | bytes 110600 | tf_op jit(solution)/shard_map/ppermute | solution.py:245
  7.1 5.7 %copy-start.14 = (f32[2,4,1152]{2,1,0:T(4,128)S(1)}, f32[2,4,1152]{2,1,0:T(4,128)}, u32[]{:S(2)}) copy-start(f32[2,4,1152]{2,1,0:T(4,128)} %get-tuple-element.22) | copy-start | bytes 110596
  9.5 19.3 %collective-permute-start.3 = (f32[64,1152]{1,0:T(8,128)}, f32[64,1152]{1,0:T(8,128)S(1)}, u32[]{:S(2)}, u32[]{:S(2)}) collective-permute-start(f32[64,1152]{1,0:T(8,128)} %get-tuple-element.26), channel_id=1, source_target_pairs={{0,8},{8,16},{16,24},{24,0},{1,9},{9,17},{17,25},{25,1},{2,10},{10... | collective-permute-start | bytes 884744 | tf_op jit(solution)/shard_map/ppermute | solution.py:245
  9.5 2.3 %copy-start.15 = (s32[4]{0:T(128)S(1)}, s32[4]{0:T(128)}, u32[]{:S(2)}) copy-start(s32[4]{0:T(128)} %param.6) | copy-start | bytes 52
  9.5 19.3 %collective-permute-start.4 = (f32[64,1152]{1,0:T(8,128)}, f32[64,1152]{1,0:T(8,128)S(1)}, u32[]{:S(2)}, u32[]{:S(2)}) collective-permute-start(f32[64,1152]{1,0:T(8,128)} %get-tuple-element.27), channel_id=1, source_target_pairs={{0,16},{8,24},{16,0},{24,8},{1,17},{9,25},{17,1},{25,9},{2,18},{10... | collective-permute-start | bytes 884744 | tf_op jit(solution)/shard_map/ppermute | solution.py:245
  11.2 17.6 %collective-permute-start.5 = (f32[64,1152]{1,0:T(8,128)}, f32[64,1152]{1,0:T(8,128)S(1)}, u32[]{:S(2)}, u32[]{:S(2)}) collective-permute-start(f32[64,1152]{1,0:T(8,128)} %get-tuple-element.28), channel_id=1, source_target_pairs={{0,24},{8,0},{16,8},{24,16},{1,25},{9,1},{17,9},{25,17},{2,26},{10... | collective-permute-start | bytes 884744 | tf_op jit(solution)/shard_map/ppermute | solution.py:245
  12.8 0.9 %copy-start.8 = (f32[2,4,1152]{2,1,0:T(4,128)}, f32[2,4,1152]{2,1,0:T(4,128)S(1)}, u32[]{:S(2)}) copy-start(f32[2,4,1152]{2,1,0:T(4,128)S(1)} %collective-permute-done.refs_1_) | copy-start | bytes 110596
  12.9 12.6 %collective-permute-start.2 = (f32[2,4,1152]{2,1,0:T(4,128)S(1)}, f32[2,4,1152]{2,1,0:T(4,128)S(1)}, u32[]{:S(2)}, u32[]{:S(2)}) collective-permute-start(f32[2,4,1152]{2,1,0:T(4,128)S(1)} %copy-done.14), channel_id=1, source_target_pairs={{0,24},{8,0},{16,8},{24,16},{1,25},{9,1},{17,9},{25,17},{2,26},{10... | collective-permute-start | bytes 110600 | tf_op jit(solution)/shard_map/ppermute | solution.py:245
  14.5 11.0 %copy-start.9 = (f32[2,4,1152]{2,1,0:T(4,128)}, f32[2,4,1152]{2,1,0:T(4,128)S(1)}, u32[]{:S(2)}) copy-start(f32[2,4,1152]{2,1,0:T(4,128)S(1)} %collective-permute-done.1.refs_2_) | copy-start | bytes 110596
  25.4 0.6 copy-start.10
  28.8 0.7 copy-start.1
  28.8 0.8 %copy-start.2 = (f32[64,1152]{1,0:T(8,128)}, f32[64,1152]{1,0:T(8,128)S(1)}, u32[]{:S(2)}) copy-start(f32[64,1152]{1,0:T(8,128)S(1)} %collective-permute-done.4.refs_2_) | copy-start | bytes 884740
  28.8 0.9 %copy-start.3 = (f32[64,1152]{1,0:T(8,128)}, f32[64,1152]{1,0:T(8,128)S(1)}, u32[]{:S(2)}) copy-start(f32[64,1152]{1,0:T(8,128)S(1)} %collective-permute-done.5.refs_3_) | copy-start | bytes 884740
  33.6 6.3 %collective-permute-start.6 = (f32[32,1152]{1,0:T(8,128)}, f32[32,1152]{1,0:T(8,128)S(1)}, u32[]{:S(2)}, u32[]{:S(2)}) collective-permute-start(f32[32,1152]{1,0:T(8,128)} %back_0.1.own), channel_id=1, source_target_pairs={{0,1},{1,2},{2,3},{3,4},{4,5},{5,6},{6,7},{8,9},{9,10},{10,11},{11... | collective-permute-start | bytes 442376 | tf_op jit(solution)/shard_map/ppermute | solution.py:253
  36.8 7.1 %collective-permute-start.7 = (f32[32,1152]{1,0:T(8,128)}, f32[32,1152]{1,0:T(8,128)S(1)}, u32[]{:S(2)}, u32[]{:S(2)}) collective-permute-start(f32[32,1152]{1,0:T(8,128)} %back_0.1.own), channel_id=1, source_target_pairs={{1,0},{2,1},{3,2},{4,3},{5,4},{6,5},{7,6},{9,8},{10,9},{11,10},{12... | collective-permute-start | bytes 442376 | tf_op jit(solution)/shard_map/ppermute | solution.py:254
  39.9 4.0 %copy-start.6 = (f32[32,1152]{1,0:T(8,128)}, f32[32,1152]{1,0:T(8,128)S(1)}, u32[]{:S(2)}) copy-start(f32[32,1152]{1,0:T(8,128)S(1)} %collective-permute-done.6.low) | copy-start | bytes 442372
  43.9 0.7 copy-start.7
  49.2 6.5 %collective-permute-start.8 = (f32[32,1152]{1,0:T(8,128)}, f32[32,1152]{1,0:T(8,128)S(1)}, u32[]{:S(2)}, u32[]{:S(2)}) collective-permute-start(f32[32,1152]{1,0:T(8,128)} %middle_1.1.own), channel_id=1, source_target_pairs={{0,1},{1,2},{2,3},{3,4},{4,5},{5,6},{6,7},{8,9},{9,10},{10,11},{11... | collective-permute-start | bytes 442376 | tf_op jit(solution)/shard_map/ppermute | solution.py:253
  53.3 6.1 %collective-permute-start.9 = (f32[32,1152]{1,0:T(8,128)}, f32[32,1152]{1,0:T(8,128)S(1)}, u32[]{:S(2)}, u32[]{:S(2)}) collective-permute-start(f32[32,1152]{1,0:T(8,128)} %middle_1.1.own), channel_id=1, source_target_pairs={{1,0},{2,1},{3,2},{4,3},{5,4},{6,5},{7,6},{9,8},{10,9},{11,10},{12... | collective-permute-start | bytes 442376 | tf_op jit(solution)/shard_map/ppermute | solution.py:254
  55.7 3.7 %copy-start.4 = (f32[32,1152]{1,0:T(8,128)}, f32[32,1152]{1,0:T(8,128)S(1)}, u32[]{:S(2)}) copy-start(f32[32,1152]{1,0:T(8,128)S(1)} %collective-permute-done.8.low) | copy-start | bytes 442372
  59.4 0.7 copy-start.5
  62.3 5.2 %collective-permute-start.10 = (f32[2,4,1024]{2,1,0:T(4,128)}, f32[2,4,1024]{2,1,0:T(4,128)S(1)}, u32[]{:S(2)}, u32[]{:S(2)}) collective-permute-start(f32[2,4,1024]{2,1,0:T(4,128)} %get-tuple-element.30), channel_id=1, source_target_pairs={{0,8},{8,16},{16,24},{24,0},{1,9},{9,17},{17,25},{25,1},{2,10},{10... | collective-permute-start | bytes 98312 | tf_op jit(solution)/shard_map/ppermute | solution.py:245
  66.2 3.0 %collective-permute-start.11 = (f32[2,4,1024]{2,1,0:T(4,128)}, f32[2,4,1024]{2,1,0:T(4,128)S(1)}, u32[]{:S(2)}, u32[]{:S(2)}) collective-permute-start(f32[2,4,1024]{2,1,0:T(4,128)} %get-tuple-element.31), channel_id=1, source_target_pairs={{0,16},{8,24},{16,0},{24,8},{1,17},{9,25},{17,1},{25,9},{2,18},{10... | collective-permute-start | bytes 98312 | tf_op jit(solution)/shard_map/ppermute | solution.py:245
  66.2 3.6 %collective-permute-start.12 = (f32[2,4,1024]{2,1,0:T(4,128)}, f32[2,4,1024]{2,1,0:T(4,128)S(1)}, u32[]{:S(2)}, u32[]{:S(2)}) collective-permute-start(f32[2,4,1024]{2,1,0:T(4,128)} %get-tuple-element.32), channel_id=1, source_target_pairs={{0,24},{8,0},{16,8},{24,16},{1,25},{9,1},{17,9},{25,17},{2,26},{10... | collective-permute-start | bytes 98312 | tf_op jit(solution)/shard_map/ppermute | solution.py:245
  67.5 2.2 %copy-start.11 = (f32[2,4,1024]{2,1,0:T(4,128)}, f32[2,4,1024]{2,1,0:T(4,128)S(1)}, u32[]{:S(2)}) copy-start(f32[2,4,1024]{2,1,0:T(4,128)S(1)} %collective-permute-done.10.refs_1_) | copy-start | bytes 98308
  69.2 0.6 copy-start.12
  69.7 0.6 copy-start.13

commit v2 on v1

v2 whole, which is shorter than its diff:
```python
import functools

import jax
import jax.numpy as jnp
from jax import lax
from jax.experimental import pallas as pl
from jax.experimental.pallas import tpu as pltpu
from jax.sharding import PartitionSpec as P

SUBSETS = 2
NANG = 3000
TV_ITERS = 2
TV_STEP = 0.05
TV_EPS = 0.5
LANES = 128
SUBLANES = 8


class Sizes:
    def __init__(self, initial, measured, ray, cuts):
        self.slices, self.strip, self.breadth = initial.shape
        self.angles = measured.shape[1]
        self.ray, self.cuts = ray, cuts
        self.rows = self.strip * ray
        self.total_slices = self.slices * cuts
        self.half = (self.rows + 1) // 2
        self.taps = 2 * self.half + 1
        reach = SUBSETS * (2 * self.half + TV_ITERS)
        self.halo_tiles = -(-2 * reach // LANES)
        self.side = self.halo_tiles * (LANES // 2)
        self.cols = self.breadth // ray
        self.local = self.cols + self.halo_tiles * LANES
        self.image = self.slices * self.rows
        self.sino = self.angles * self.slices
        self.scale = 1.0 / (self.rows * self.angles)
        self.xor_ray = ray & (ray - 1) == 0
        self.paired = cuts % 2 == 0 and ray % 2 == 0
        self.keep = 8 * self.taps * self.image * self.local < 16 * 2**20

    def peer(self, place, step):
        return place ^ step if self.xor_ray else lax.rem(place + step, self.ray)

    def source(self, place, step):
        return place ^ step if self.xor_ray else lax.rem(place - step + self.ray, self.ray)

    def step_from(self, place, source):
        return place ^ source if self.xor_ray else lax.rem(place - source + self.ray, self.ray)


def iota(shape, dim):
    return lax.broadcasted_iota(jnp.int32, shape, dim)


def inside_image(z, shape):
    lane = iota(shape, len(shape) - 1)
    offset = jnp.where(lane < z.cols + z.side, lane, lane - z.local)
    column = lax.axis_index("ray") * z.cols + offset
    return column, (column >= 0) & (column < z.breadth)


def window(z, load, target):
    base = target * z.cols
    parts = [load(pl.multiple_of(base, LANES), z.cols)]
    last = z.breadth - LANES
    for j in range(z.halo_tiles):
        right = base + z.cols + j * LANES
        left = base + (j - z.halo_tiles) * LANES
        tile_r = load(pl.multiple_of(jnp.minimum(right, last), LANES), LANES)
        tile_l = load(pl.multiple_of(jnp.maximum(left, 0), LANES), LANES)
        tile_r = jnp.where(right <= last, tile_r, 0.0)
        tile_l = jnp.where(left >= 0, tile_l, 0.0)
        lane = j * LANES + iota(tile_r.shape, tile_r.ndim - 1)
        parts.append(jnp.where(lane < z.side, tile_r, tile_l))
    return jnp.concatenate(parts, axis=-1)


def split(value):
    high = value.astype(jnp.bfloat16)
    return high, (value - high.astype(jnp.float32)).astype(jnp.bfloat16)


def slopes_of(z, table, slot):
    index = table[...]
    kept = jnp.where(iota(index.shape, 0) == slot, index, 0)
    row = jnp.sum(kept, axis=0, keepdims=True).astype(jnp.float32)
    return -1.0 + (2.0 * row + 1.0) / NANG


def tent(distance):
    return jnp.maximum(1.0 - jnp.abs(distance), 0.0)


def centred(z, row):
    return row.astype(jnp.float32) - (z.rows - 1) / 2.0


def project(z, x, slopes, taps_ref):
    both = 2 * z.image
    x_high, x_low = split(x)
    stacked = jnp.concatenate([x_high, x_low], axis=0)
    for k in range(z.taps):
        shift = (z.half - k) % z.local
        rolled = pltpu.roll(stacked, shift, 1) if shift else stacked
        taps_ref[k * both : (k + 1) * both, :] = rolled
    square = (z.angles, z.angles)
    column = jnp.where(iota(square, 0) == iota(square, 1), slopes, 0.0)
    column = jnp.sum(column, axis=1, keepdims=True)
    column = jnp.concatenate([column] * z.slices, axis=0)
    group = max(1, LANES // both)
    shape = (z.sino, group * both)
    line, lane = iota(shape, 0), iota(shape, 1)
    same = line // z.angles == lax.rem(lane // z.rows, z.slices)
    distance = column * centred(z, lax.rem(lane, z.rows)) + (lane // both).astype(jnp.float32)
    distance = jnp.where(same, distance, 4.0 * z.rows)
    on_high = lax.rem(lane // z.image, 2) == 0
    highs, lows = [], []
    for first in range(0, z.taps, group):
        w_high, w_low = split(tent(distance + float(first - z.half)))
        w_low = jnp.where(on_high, w_low, jnp.zeros_like(w_low))
        keep = min(group, z.taps - first) * both
        highs.append(w_high[:, :keep])
        lows.append(w_low[:, :keep])
    weights = jnp.concatenate(
        [jnp.concatenate(highs, axis=1), jnp.concatenate(lows, axis=1)], axis=0
    )
    result = jnp.dot(weights, taps_ref[...], preferred_element_type=jnp.float32)
    return result[: z.sino] + result[z.sino :]


def back_weights(z, slopes):
    row = jnp.concatenate([slopes] * (2 * z.slices), axis=1)
    shape = (z.image, 2 * z.sino)
    line, lane = iota(shape, 0), iota(shape, 1)
    same = line // z.rows == lax.rem(lane // z.angles, z.slices)
    distance = jnp.where(same, row * centred(z, lax.rem(line, z.rows)), 4.0 * z.rows)
    parts = []
    for k in range(z.taps):
        w_high, w_low = split(tent(distance + float(k - z.half)))
        parts.append(jnp.concatenate([w_high, w_low[:, : z.sino]], axis=1))
    return jnp.concatenate(parts, axis=0)


def back(z, residual, weights, taps_ref):
    r_high, r_low = split(residual)
    stacked = jnp.concatenate([r_high, r_low, r_high], axis=0)
    taps_ref[...] = jnp.dot(weights, stacked, preferred_element_type=jnp.float32)
    tiles = []
    for first in range(0, z.image, SUBLANES):
        total = None
        for k in range(z.taps):
            at = k * z.image + first
            term = taps_ref[at : at + SUBLANES, :]
            shift = (k - z.half) % z.local
            term = pltpu.roll(term, shift, 1) if shift else term
            total = term if total is None else total + term
        tiles.append(total)
    return jnp.concatenate(tiles, axis=0)


def tv_steps(z, slabs):
    shape = slabs[0].shape
    column, inside = inside_image(z, shape)
    open_c = inside & (column < z.breadth - 1)
    open_r = iota(shape, 0) < z.rows - 1
    first_own = lax.axis_index("cuts") == 0
    last_own = lax.axis_index("cuts") == z.cuts - 1
    for turn in range(TV_ITERS):
        before = TV_ITERS - 1 - turn
        flows = []
        for k in range(len(slabs) - 1):
            here = slabs[k]
            step_s = slabs[k + 1] - here
            if k == before:
                step_s = jnp.where(first_own, 0.0, step_s)
            if k == before + z.slices:
                step_s = jnp.where(last_own, 0.0, step_s)
            step_r = jnp.where(open_r, pltpu.roll(here, z.rows - 1, 0) - here, 0.0)
            step_c = jnp.where(open_c, pltpu.roll(here, z.local - 1, 1) - here, 0.0)
            scale = lax.rsqrt(
                step_s * step_s + step_r * step_r + step_c * step_c + TV_EPS * TV_EPS
            )
            flows.append((step_s * scale, step_r * scale, step_c * scale))
        done = []
        for k in range(1, len(slabs) - 1):
            flow_s, flow_r, flow_c = flows[k]
            spread = flow_s - flows[k - 1][0]
            spread = spread + flow_r - pltpu.roll(flow_r, 1, 0)
            spread = spread + flow_c - pltpu.roll(flow_c, 1, 1)
            done.append(slabs[k] + TV_STEP * spread)
        slabs = done
    return [jnp.where(inside, slab, 0.0) for slab in slabs]


def tv_all(z, own, first, second):
    def slab(ref, s):
        return ref[s * z.rows : (s + 1) * z.rows, :]

    odd = lax.rem(lax.axis_index("cuts"), 2) == 1

    def side(one, two, s):
        if not z.paired:
            return slab(one, s)
        return jnp.where(odd, slab(one, s), slab(two, s))

    low = [side(first, second, s) for s in range(z.slices - TV_ITERS, z.slices)]
    high = [side(second, first, s) for s in range(TV_ITERS)]
    return tv_steps(z, low + [slab(own, s) for s in range(z.slices)] + high)


def measured_back(z, steps, measured, table, outs, taps_ref):
    place = lax.axis_index("ray")
    weights = back_weights(z, slopes_of(z, table, place))
    for step, out in zip(steps, outs):
        target = z.peer(place, step)
        lines = [
            window(z, lambda at, size, s=s: measured[0, :, s, pl.ds(at, size)], target)
            for s in range(z.slices)
        ]
        out[...] = back(z, jnp.concatenate(lines, axis=0), weights, taps_ref)


def start_kernel(z, steps, initial, measured, table, *refs):
    strips, outs, taps_ref = refs[: z.ray], refs[z.ray : -1], refs[-1]
    place = lax.axis_index("ray")
    for step, out in enumerate(strips):
        out[...] = window(
            z, lambda at, size: initial[:, :, pl.ds(at, size)], z.peer(place, step)
        )
    measured_back(z, steps, measured, table, outs, taps_ref)


def more_kernel(z, steps, measured, table, *refs):
    measured_back(z, steps, measured, table, refs[:-1], refs[-1])


def modelled_update(z, slot, table, x, x_taps, r_taps):
    slopes = slopes_of(z, table, slot)
    forward = project(z, x, slopes, x_taps)
    _, inside = inside_image(z, forward.shape)
    forward = jnp.where(inside, forward, 0.0)
    return x - back(z, forward, back_weights(z, slopes), r_taps) * z.scale


def add_measured(z, slot, stored, value, out):
    wanted = z.step_from(lax.axis_index("ray"), slot)
    for step, piece in enumerate(stored):

        @pl.when(wanted == step)
        def _():
            out[...] = value + piece[...] * z.scale


def first_kernel(z, order, table, *refs):
    pieces, (out, strips, x_taps, r_taps) = refs[: z.ray], refs[z.ray :]
    place = lax.axis_index("ray")
    for step, piece in enumerate(pieces):
        strips[z.source(place, step)] = piece[...]
    x = jnp.concatenate(
        [strips[r, s] for s in range(z.slices) for r in range(z.ray)], axis=0
    )
    out[...] = modelled_update(z, order[0], table, x, x_taps, r_taps)


def add_kernel(z, order, value, *refs):
    add_measured(z, order[0], refs[: z.ray], value[...], refs[z.ray])


def middle_kernel(z, subset, order, table, own, first, second, *refs):
    stored, (out, x_taps, r_taps) = refs[: z.ray], refs[z.ray :]
    x = jnp.concatenate(tv_all(z, own, first, second), axis=0)
    value = modelled_update(z, order[subset], table, x, x_taps, r_taps)
    add_measured(z, order[subset], stored, value, out)


def last_kernel(z, own, first, second, *refs):
    outs, rows = refs[: z.ray], refs[z.ray]
    for s, slab in enumerate(tv_all(z, own, first, second)):
        for r in range(z.ray):
            rows[r, s] = slab[r * z.strip : (r + 1) * z.strip, : z.cols]
    place = lax.axis_index("ray")
    for step, out in enumerate(outs):
        out[...] = rows[z.peer(place, step)]


def join_kernel(z, *refs):
    pieces, out = refs[: z.ray], refs[z.ray]
    place = lax.axis_index("ray")
    for step, piece in enumerate(pieces):
        at = pl.multiple_of(z.source(place, step) * z.cols, LANES)
        out[:, :, pl.ds(at, z.cols)] = piece[...]


def call(kernel, name, outs, operands, kinds, scratch=(), keep=True):
    keep = keep and kernel.args[0].keep
    single = isinstance(outs[0], int)
    shapes = [outs] if single else list(outs)
    make = pltpu.VMEM if keep else jax.ShapeDtypeStruct
    operands = [
        pltpu.with_memory_space_constraint(value, pltpu.VMEM)
        if kind == "v" and kernel.args[0].keep
        else value
        for value, kind in zip(operands, kinds)
    ]
    result = pl.pallas_call(
        kernel,
        name=name,
        out_shape=[make(shape, jnp.float32) for shape in shapes],
        in_specs=[
            pl.BlockSpec(memory_space=pltpu.SMEM if kind == "s" else pltpu.VMEM)
            for kind in kinds
        ],
        out_specs=[pl.BlockSpec(memory_space=pltpu.VMEM) for _ in shapes],
        scratch_shapes=list(scratch),
    )(*operands)
    return result[0] if single else result


def swap_over_ray(z, pieces, steps):
    got = []
    for step, piece in zip(steps, pieces):
        if step == 0:
            got.append(piece)
            continue
        if z.xor_ray:
            pairs = [(i, i ^ step) for i in range(z.ray)]
        else:
            pairs = [(i, (i + step) % z.ray) for i in range(z.ray)]
        got.append(lax.ppermute(piece, "ray", pairs))
    return got


def neighbours(z, x):
    if not z.paired:
        up = [(i, i + 1) for i in range(z.cuts - 1)]
        down = [(i + 1, i) for i in range(z.cuts - 1)]
        return lax.ppermute(x, "cuts", up), lax.ppermute(x, "cuts", down)
    even = [(c, c ^ 1) for c in range(z.cuts)]
    odd = []
    for r in range(z.ray):
        for c in range(z.cuts):
            if c in (0, z.cuts - 1):
                to = (r ^ 1) * z.cuts + c
            else:
                to = r * z.cuts + (c + 1 if c % 2 else c - 1)
            odd.append((r * z.cuts + c, to))
    return lax.ppermute(x, "cuts", even), lax.ppermute(x, ("ray", "cuts"), odd)


def on_device(ray, cuts, initial, measured, order, angle_index):
    z = Sizes(initial, measured, ray, cuts)
    bind = lambda kernel, *more: functools.partial(kernel, z, *more)
    whole = (z.image, z.local)
    x_taps = pltpu.VMEM((2 * z.taps * z.image, z.local), jnp.bfloat16)
    r_taps = pltpu.VMEM((z.taps * z.image, z.local), jnp.float32)

    steps = list(range(2, ray)) + list(range(min(2, ray)))
    head, tail = steps[:2], steps[2:]
    outs = call(
        bind(start_kernel, head),
        "start",
        [(z.slices, z.strip, z.local)] * ray + [whole] * len(head),
        [initial, measured, angle_index],
        "ppp",
        [r_taps],
    )
    strips = swap_over_ray(z, outs[:ray], range(ray))
    stored = dict(zip(head, swap_over_ray(z, outs[ray:], head)))
    while tail:
        head, tail = tail[:2], tail[2:]
        outs = call(
            bind(more_kernel, head),
            "more",
            [whole] * len(head),
            [measured, angle_index],
            "pp",
            [r_taps],
        )
        stored.update(zip(head, swap_over_ray(z, outs, head)))
    stored = [stored[step] for step in range(ray)]

    value = call(
        bind(first_kernel),
        "first",
        whole,
        [order, angle_index, *strips],
        "sp" + "v" * ray,
        [pltpu.VMEM((ray, z.slices, z.strip, z.local), jnp.float32), x_taps, r_taps],
    )
    x = call(bind(add_kernel), "add", whole, [order, value, *stored], "sv" + "v" * ray)
    for subset in range(1, SUBSETS):
        x = call(
            bind(middle_kernel, subset),
            f"middle_{subset}",
            whole,
            [order, angle_index, x, *neighbours(z, x), *stored],
            "spvvv" + "v" * ray,
            [x_taps, r_taps],
        )
    pieces = call(
        bind(last_kernel),
        "last",
        [(z.slices, z.strip, z.cols)] * ray,
        [x, *neighbours(z, x)],
        "vvv",
        [pltpu.VMEM((ray, z.slices, z.strip, z.cols), jnp.float32)],
    )
    return call(
        bind(join_kernel),
        "join",
        (z.slices, z.strip, z.breadth),
        swap_over_ray(z, pieces, range(ray)),
        "v" * ray,
        keep=False,
    )


def solution(mesh):
    return jax.shard_map(
        functools.partial(on_device, mesh.shape["ray"], mesh.shape["cuts"]),
        mesh=mesh,
        in_specs=(P("cuts", "ray", None), P("ray", None, "cuts", None), P(), P()),
        out_specs=P("cuts", "ray", None),
        check_vma=False,
    )
```

time: 73 us -> 50.1 us (0.69)
  local copies, waits for them, and re-layouts: 9.96 us -> 0 us
  Pallas kernels: 18.9 us -> 13.6 us
  starting transfers between devices: 19 us -> 14.3 us
  waiting for transfers between devices: 23.2 us -> 21.6 us
    pallas_call x7, Pallas kernels: 18.9 us -> 13.6 us  [call(): pl.pallas_call(kernel, name=name, out_shape=[make(shape, jnp.float32) for...]
    ppermute x13, starting transfers between devices: 19 us -> 14.3 us  [the longest x9 8.09 us: swap_over_ray(): got.append(lax.ppermute(piece, 'ray', pairs))]
    unnamed x32 -> x0, local copies, waits for them, and re-layouts: 3.47 us -> none
    reshape x1 -> x0, local copies, waits for them, and re-layouts: 2.93 us -> none  [on_device(): lines = measured.reshape(z.sino, z.breadth)]
    broadcast_in_dim x6 -> x0, local copies, waits for them, and re-layouts: 1.7 us -> none  [on_device(): slopes = jnp.repeat(slopes, z.slices, axis=1)]
    ppermute x13, waiting for transfers between devices: 23.2 us -> 21.6 us  [the longest x2 12.7 us: neighbours(): lax.ppermute(x, 'cuts', even)]
    another operation x4 -> x0, local copies, waits for them, and re-layouts: 1.29 us -> none  [on_device(): slope_row = jnp.tile(slopes, (1, 3))[:, None, :]]
  transfers between devices with their start and end apart: 13 -> 13, of which waited for: 8 -> 6; matrix products, arithmetic and copies ran while one was open for 10% -> 0% of each run, Pallas kernels for 7% -> 11%
where the time goes in v2:
time: 50.1 us; the launch traced here: 49.6 us
  waiting for transfers between devices  21.6 us (43%)
  starting transfers between devices  14.3 us (29%)
  Pallas kernels  13.6 us (27%)
    pallas_call x7, Pallas kernels, call(): pl.pallas_call(kernel, name=name, out_shape=[make(shape, jnp.float32) for...  13.6 us
    ppermute x2, waiting for transfers between devices, neighbours(): lax.ppermute(x, 'cuts', even)  12.7 us
    ppermute x9, waiting for transfers between devices, swap_over_ray(): got.append(lax.ppermute(piece, 'ray', pairs))  8.86 us
    ppermute x9, starting transfers between devices, swap_over_ray(): got.append(lax.ppermute(piece, 'ray', pairs))  8.09 us
    ppermute x2, starting transfers between devices, neighbours(): lax.ppermute(x, 'cuts', even)  5.22 us
    ppermute x2, starting transfers between devices, neighbours(): lax.ppermute(x, ('ray', 'cuts'), odd)  1.02 us
  transfers between devices with their start and end apart: 13, of which 6 were waited for; matrix products, arithmetic and copies ran while one was open for 0% of the time, Pallas kernels for 11%

profile of v2, /device:TPU:1, one launch (start us, length us, event | category | flops | bytes accessed | tf_op | source)
XLA Modules:
  0.0 49.6 jit_solution(1713425104205799234)
XLA Ops:
  0.0 3.0 %more.1 = (f32[32,1152]{1,0:T(8,128)S(1)}, f32[32,1152]{1,0:T(8,128)S(1)}) custom-call(f32[1,32,2,4096]{3,2,1,0:T(2,128)} %measured.3, s32[4,32]{1,0:T(4,128)} %table.7), custom_call_target="tpu_custom_call" | custom-call | tf_op jit(solution)/shard_map/more/pallas_call | solution.py:304
  3.0 0.1 collective-permute-start.3
  3.1 3.0 %start.1 = (f32[2,4,1152]{2,1,0:T(4,128)S(1)}, f32[2,4,1152]{2,1,0:T(4,128)S(1)}, f32[2,4,1152]{2,1,0:T(4,128)S(1)}, f32[2,4,1152]{2,1,0:T(4,128)S(1)}, f32[32,1152]{1,0:T(8,128)S(1)}, /*index=5*/f32[32,1152]{1,0:T(8,128)S(1)}) custom-call(f32[2,4,4096]{2,1,0:T(4,128)} %initial.1, f32[1,32,2,4096]{3,2,1,0:T(2,128)} %measured.3, s32[4,32]{1,0:T(4,128)} %table.7), custom_call_target="tpu_custom_call" | custom-call | tf_op jit(solution)/shard_map/start/pallas_call | solution.py:304
  6.1 2.8 %collective-permute-start.4 = (f32[32,1152]{1,0:T(8,128)S(1)}, f32[32,1152]{1,0:T(8,128)S(1)}, u32[]{:S(2)}, u32[]{:S(2)}) collective-permute-start(f32[32,1152]{1,0:T(8,128)S(1)} %get-tuple-element.23), channel_id=1, source_target_pairs={{0,16},{8,24},{16,0},{24,8},{1,17},{9,25},{17,1},{25,9},{2,18},{10... | collective-permute-start | bytes 442376 | tf_op jit(solution)/shard_map/ppermute | solution.py:328
  8.9 0.0 collective-permute-start.5
  8.9 0.5 collective-permute-start
  9.4 1.4 %collective-permute-start.1 = (f32[2,4,1152]{2,1,0:T(4,128)S(1)}, f32[2,4,1152]{2,1,0:T(4,128)S(1)}, u32[]{:S(2)}, u32[]{:S(2)}) collective-permute-start(f32[2,4,1152]{2,1,0:T(4,128)S(1)} %get-tuple-element.19), channel_id=1, source_target_pairs={{0,16},{8,24},{16,0},{24,8},{1,17},{9,25},{17,1},{25,9},{2,18},{10... | collective-permute-start | bytes 110600 | tf_op jit(solution)/shard_map/ppermute | solution.py:328
  10.8 0.0 collective-permute-done.refs_1_
  10.8 1.1 %collective-permute-start.2 = (f32[2,4,1152]{2,1,0:T(4,128)S(1)}, f32[2,4,1152]{2,1,0:T(4,128)S(1)}, u32[]{:S(2)}, u32[]{:S(2)}) collective-permute-start(f32[2,4,1152]{2,1,0:T(4,128)S(1)} %get-tuple-element.20), channel_id=1, source_target_pairs={{0,24},{8,16},{16,8},{24,0},{1,25},{9,17},{17,9},{25,1},{2,26},{10... | collective-permute-start | bytes 110600 | tf_op jit(solution)/shard_map/ppermute | solution.py:328
  11.9 5.2 %collective-permute-done.1.refs_2_ = f32[2,4,1152]{2,1,0:T(4,128)S(1)} collective-permute-done((f32[2,4,1152]{2,1,0:T(4,128)S(1)}, f32[2,4,1152]{2,1,0:T(4,128)S(1)}, u32[]{:S(2)}, u32[]{:S(2)}) %collective-permute-start.1) | collective-permute-done | bytes 36896 | tf_op jit(solution)/shard_map/ppermute | solution.py:328
  17.0 0.8 %collective-permute-done.2.refs_3_ = f32[2,4,1152]{2,1,0:T(4,128)S(1)} collective-permute-done((f32[2,4,1152]{2,1,0:T(4,128)S(1)}, f32[2,4,1152]{2,1,0:T(4,128)S(1)}, u32[]{:S(2)}, u32[]{:S(2)}) %collective-permute-start.2) | collective-permute-done | bytes 36896 | tf_op jit(solution)/shard_map/ppermute | solution.py:328
  17.8 2.6 %first.1.value = f32[32,1152]{1,0:T(8,128)S(1)} custom-call(s32[4]{0:T(128)} %order.5, s32[4,32]{1,0:T(4,128)} %table.7, f32[2,4,1152]{2,1,0:T(4,128)S(1)} %get-tuple-element.17.refs_0_, f32[2,4,1152]{2,1,0:T(4,128)S(1)} %collective-permute-done.refs_1_, f32[2,4,1152]{2,1,0:T(4,128)S(1)} %collective-permute-done.1.refs_2_, ...), custom_call_target="tpu_custom_call" | custom-call | tf_op jit(solution)/shard_map/first/pallas_call | solution.py:304
  20.4 0.0 collective-permute-done.3.refs_1_
  20.4 0.0 collective-permute-done.4.refs_2_
  20.4 0.0 collective-permute-done.5.refs_3_
  20.4 0.7 %add.1.own = f32[32,1152]{1,0:T(8,128)S(1)} custom-call(s32[4]{0:T(128)} %order.5, f32[32,1152]{1,0:T(8,128)S(1)} %first.1.value, f32[32,1152]{1,0:T(8,128)S(1)} %get-tuple-element.21.refs_0_, f32[32,1152]{1,0:T(8,128)S(1)} %collective-permute-done.3.refs_1_, f32[32,1152]{1,0:T(8,128)S(1)} %collective-permute-done.4.refs_2_, ...), custom_call_target="tpu_custom_call" | custom-call | tf_op jit(solution)/shard_map/add/pallas_call | solution.py:304
  21.1 0.5 collective-permute-start.7
  21.6 2.2 %collective-permute-start.6 = (f32[32,1152]{1,0:T(8,128)S(1)}, f32[32,1152]{1,0:T(8,128)S(1)}, u32[]{:S(2)}, u32[]{:S(2)}) collective-permute-start(f32[32,1152]{1,0:T(8,128)S(1)} %add.1.own), channel_id=1, source_target_pairs={{0,1},{1,0},{2,3},{3,2},{4,5},{5,4},{6,7},{7,6},{8,9},{9,8},{10,11... | collective-permute-start | bytes 442376 | tf_op jit(solution)/shard_map/ppermute | solution.py:346
  23.8 0.0 collective-permute-done.7.second
  23.8 6.4 %collective-permute-done.6.first = f32[32,1152]{1,0:T(8,128)S(1)} collective-permute-done((f32[32,1152]{1,0:T(8,128)S(1)}, f32[32,1152]{1,0:T(8,128)S(1)}, u32[]{:S(2)}, u32[]{:S(2)}) %collective-permute-start.6) | collective-permute-done | bytes 147488 | tf_op jit(solution)/shard_map/ppermute | solution.py:346
  30.2 3.1 %middle_1.1.own = f32[32,1152]{1,0:T(8,128)S(1)} custom-call(s32[4]{0:T(128)} %order.5, s32[4,32]{1,0:T(4,128)} %table.7, f32[32,1152]{1,0:T(8,128)S(1)} %add.1.own, f32[32,1152]{1,0:T(8,128)S(1)} %collective-permute-done.6.first, f32[32,1152]{1,0:T(8,128)S(1)} %collective-permute-done.7.second, f32[32,1152]{1,0:T(8,128)S(1)} %get-tuple-element.21.refs_0_, ...), custom_call_target="tpu_custom_call" | custom-call | tf_op jit(solution)/shard_map/middle_1/pallas_call | solution.py:304
  33.3 0.6 %collective-permute-start.9 = (f32[32,1152]{1,0:T(8,128)S(1)}, f32[32,1152]{1,0:T(8,128)S(1)}, u32[]{:S(2)}, u32[]{:S(2)}) collective-permute-start(f32[32,1152]{1,0:T(8,128)S(1)} %middle_1.1.own), channel_id=1, source_target_pairs={{0,8},{1,2},{2,1},{3,4},{4,3},{5,6},{6,5},{7,15},{8,0},{9,10},{10,... | collective-permute-start | bytes 442376 | tf_op jit(solution)/shard_map/ppermute | solution.py:346
  33.9 3.0 %collective-permute-start.8 = (f32[32,1152]{1,0:T(8,128)S(1)}, f32[32,1152]{1,0:T(8,128)S(1)}, u32[]{:S(2)}, u32[]{:S(2)}) collective-permute-start(f32[32,1152]{1,0:T(8,128)S(1)} %middle_1.1.own), channel_id=1, source_target_pairs={{0,1},{1,0},{2,3},{3,2},{4,5},{5,4},{6,7},{7,6},{8,9},{9,8},{10,11... | collective-permute-start | bytes 442376 | tf_op jit(solution)/shard_map/ppermute | solution.py:346
  36.8 0.0 collective-permute-done.9.second
  36.8 6.4 %collective-permute-done.8.first = f32[32,1152]{1,0:T(8,128)S(1)} collective-permute-done((f32[32,1152]{1,0:T(8,128)S(1)}, f32[32,1152]{1,0:T(8,128)S(1)}, u32[]{:S(2)}, u32[]{:S(2)}) %collective-permute-start.8) | collective-permute-done | bytes 147488 | tf_op jit(solution)/shard_map/ppermute | solution.py:346
  43.2 0.5 %last.1 = (f32[2,4,1024]{2,1,0:T(4,128)S(1)}, f32[2,4,1024]{2,1,0:T(4,128)S(1)}, f32[2,4,1024]{2,1,0:T(4,128)S(1)}, f32[2,4,1024]{2,1,0:T(4,128)S(1)}) custom-call(f32[32,1152]{1,0:T(8,128)S(1)} %middle_1.1.own, f32[32,1152]{1,0:T(8,128)S(1)} %collective-permute-done.8.first, f32[32,1152]{1,0:T(8,128)S(1)} %collective-permute-done.9.second), custom_call_target="tpu_custom_call" | custom-call | tf_op jit(solution)/shard_map/last/pallas_call | solution.py:304
  43.7 0.6 %collective-permute-start.10 = (f32[2,4,1024]{2,1,0:T(4,128)S(1)}, f32[2,4,1024]{2,1,0:T(4,128)S(1)}, u32[]{:S(2)}, u32[]{:S(2)}) collective-permute-start(f32[2,4,1024]{2,1,0:T(4,128)S(1)} %get-tuple-element.26), channel_id=1, source_target_pairs={{0,8},{8,0},{16,24},{24,16},{1,9},{9,1},{17,25},{25,17},{2,10},{10... | collective-permute-start | bytes 98312 | tf_op jit(solution)/shard_map/ppermute | solution.py:328
  44.3 1.2 %collective-permute-start.11 = (f32[2,4,1024]{2,1,0:T(4,128)S(1)}, f32[2,4,1024]{2,1,0:T(4,128)S(1)}, u32[]{:S(2)}, u32[]{:S(2)}) collective-permute-start(f32[2,4,1024]{2,1,0:T(4,128)S(1)} %get-tuple-element.27), channel_id=1, source_target_pairs={{0,16},{8,24},{16,0},{24,8},{1,17},{9,25},{17,1},{25,9},{2,18},{10... | collective-permute-start | bytes 98312 | tf_op jit(solution)/shard_map/ppermute | solution.py:328
  45.5 0.5 collective-permute-start.12
  46.0 1.1 %collective-permute-done.11.refs_2_ = f32[2,4,1024]{2,1,0:T(4,128)S(1)} collective-permute-done((f32[2,4,1024]{2,1,0:T(4,128)S(1)}, f32[2,4,1024]{2,1,0:T(4,128)S(1)}, u32[]{:S(2)}, u32[]{:S(2)}) %collective-permute-start.11) | collective-permute-done | bytes 32800 | tf_op jit(solution)/shard_map/ppermute | solution.py:328
  47.1 1.8 %collective-permute-done.12.refs_3_ = f32[2,4,1024]{2,1,0:T(4,128)S(1)} collective-permute-done((f32[2,4,1024]{2,1,0:T(4,128)S(1)}, f32[2,4,1024]{2,1,0:T(4,128)S(1)}, u32[]{:S(2)}, u32[]{:S(2)}) %collective-permute-start.12) | collective-permute-done | bytes 32800 | tf_op jit(solution)/shard_map/ppermute | solution.py:328
  48.9 0.7 %join.1 = f32[2,4,4096]{2,1,0:T(4,128)} custom-call(f32[2,4,1024]{2,1,0:T(4,128)S(1)} %get-tuple-element.25.refs_0_, f32[2,4,1024]{2,1,0:T(4,128)S(1)} %collective-permute-done.10.refs_1_, f32[2,4,1024]{2,1,0:T(4,128)S(1)} %collective-permute-done.11.refs_2_, f32[2,4,1024]{2,1,0:T(4,128)S(1)} %collective-permute-done.12.refs_3_), custom_call_target="tpu_custom_call" | custom-call | tf_op jit(solution)/shard_map/join/pallas_call | solution.py:304
  (1 shorter events, 0.0 us)
Async XLA Ops:
  3.0 17.4 %collective-permute-start.3 = (f32[32,1152]{1,0:T(8,128)S(1)}, f32[32,1152]{1,0:T(8,128)S(1)}, u32[]{:S(2)}, u32[]{:S(2)}) collective-permute-start(f32[32,1152]{1,0:T(8,128)S(1)} %get-tuple-element.22), channel_id=1, source_target_pairs={{0,8},{8,0},{16,24},{24,16},{1,9},{9,1},{17,25},{25,17},{2,10},{10... | collective-permute-start | bytes 442376 | tf_op jit(solution)/shard_map/ppermute | solution.py:328
  6.1 14.3 %collective-permute-start.4 = (f32[32,1152]{1,0:T(8,128)S(1)}, f32[32,1152]{1,0:T(8,128)S(1)}, u32[]{:S(2)}, u32[]{:S(2)}) collective-permute-start(f32[32,1152]{1,0:T(8,128)S(1)} %get-tuple-element.23), channel_id=1, source_target_pairs={{0,16},{8,24},{16,0},{24,8},{1,17},{9,25},{17,1},{25,9},{2,18},{10... | collective-permute-start | bytes 442376 | tf_op jit(solution)/shard_map/ppermute | solution.py:328
  8.9 11.5 %collective-permute-start.5 = (f32[32,1152]{1,0:T(8,128)S(1)}, f32[32,1152]{1,0:T(8,128)S(1)}, u32[]{:S(2)}, u32[]{:S(2)}) collective-permute-start(f32[32,1152]{1,0:T(8,128)S(1)} %get-tuple-element.24), channel_id=1, source_target_pairs={{0,24},{8,16},{16,8},{24,0},{1,25},{9,17},{17,9},{25,1},{2,26},{10... | collective-permute-start | bytes 442376 | tf_op jit(solution)/shard_map/ppermute | solution.py:328
  8.9 1.9 %collective-permute-start = (f32[2,4,1152]{2,1,0:T(4,128)S(1)}, f32[2,4,1152]{2,1,0:T(4,128)S(1)}, u32[]{:S(2)}, u32[]{:S(2)}) collective-permute-start(f32[2,4,1152]{2,1,0:T(4,128)S(1)} %get-tuple-element.18), channel_id=1, source_target_pairs={{0,8},{8,0},{16,24},{24,16},{1,9},{9,1},{17,25},{25,17},{2,10},{10... | collective-permute-start | bytes 110600 | tf_op jit(solution)/shard_map/ppermute | solution.py:328
  9.4 7.7 %collective-permute-start.1 = (f32[2,4,1152]{2,1,0:T(4,128)S(1)}, f32[2,4,1152]{2,1,0:T(4,128)S(1)}, u32[]{:S(2)}, u32[]{:S(2)}) collective-permute-start(f32[2,4,1152]{2,1,0:T(4,128)S(1)} %get-tuple-element.19), channel_id=1, source_target_pairs={{0,16},{8,24},{16,0},{24,8},{1,17},{9,25},{17,1},{25,9},{2,18},{10... | collective-permute-start | bytes 110600 | tf_op jit(solution)/shard_map/ppermute | solution.py:328
  10.8 7.1 %collective-permute-start.2 = (f32[2,4,1152]{2,1,0:T(4,128)S(1)}, f32[2,4,1152]{2,1,0:T(4,128)S(1)}, u32[]{:S(2)}, u32[]{:S(2)}) collective-permute-start(f32[2,4,1152]{2,1,0:T(4,128)S(1)} %get-tuple-element.20), channel_id=1, source_target_pairs={{0,24},{8,16},{16,8},{24,0},{1,25},{9,17},{17,9},{25,1},{2,26},{10... | collective-permute-start | bytes 110600 | tf_op jit(solution)/shard_map/ppermute | solution.py:328
  21.1 2.7 %collective-permute-start.7 = (f32[32,1152]{1,0:T(8,128)S(1)}, f32[32,1152]{1,0:T(8,128)S(1)}, u32[]{:S(2)}, u32[]{:S(2)}) collective-permute-start(f32[32,1152]{1,0:T(8,128)S(1)} %add.1.own), channel_id=1, source_target_pairs={{0,8},{1,2},{2,1},{3,4},{4,3},{5,6},{6,5},{7,15},{8,0},{9,10},{10,... | collective-permute-start | bytes 442376 | tf_op jit(solution)/shard_map/ppermute | solution.py:346
  21.6 8.6 %collective-permute-start.6 = (f32[32,1152]{1,0:T(8,128)S(1)}, f32[32,1152]{1,0:T(8,128)S(1)}, u32[]{:S(2)}, u32[]{:S(2)}) collective-permute-start(f32[32,1152]{1,0:T(8,128)S(1)} %add.1.own), channel_id=1, source_target_pairs={{0,1},{1,0},{2,3},{3,2},{4,5},{5,4},{6,7},{7,6},{8,9},{9,8},{10,11... | collective-permute-start | bytes 442376 | tf_op jit(solution)/shard_map/ppermute | solution.py:346
  33.3 3.5 %collective-permute-start.9 = (f32[32,1152]{1,0:T(8,128)S(1)}, f32[32,1152]{1,0:T(8,128)S(1)}, u32[]{:S(2)}, u32[]{:S(2)}) collective-permute-start(f32[32,1152]{1,0:T(8,128)S(1)} %middle_1.1.own), channel_id=1, source_target_pairs={{0,8},{1,2},{2,1},{3,4},{4,3},{5,6},{6,5},{7,15},{8,0},{9,10},{10,... | collective-permute-start | bytes 442376 | tf_op jit(solution)/shard_map/ppermute | solution.py:346
  33.9 9.3 %collective-permute-start.8 = (f32[32,1152]{1,0:T(8,128)S(1)}, f32[32,1152]{1,0:T(8,128)S(1)}, u32[]{:S(2)}, u32[]{:S(2)}) collective-permute-start(f32[32,1152]{1,0:T(8,128)S(1)} %middle_1.1.own), channel_id=1, source_target_pairs={{0,1},{1,0},{2,3},{3,2},{4,5},{5,4},{6,7},{7,6},{8,9},{9,8},{10,11... | collective-permute-start | bytes 442376 | tf_op jit(solution)/shard_map/ppermute | solution.py:346
  43.7 2.3 %collective-permute-start.10 = (f32[2,4,1024]{2,1,0:T(4,128)S(1)}, f32[2,4,1024]{2,1,0:T(4,128)S(1)}, u32[]{:S(2)}, u32[]{:S(2)}) collective-permute-start(f32[2,4,1024]{2,1,0:T(4,128)S(1)} %get-tuple-element.26), channel_id=1, source_target_pairs={{0,8},{8,0},{16,24},{24,16},{1,9},{9,1},{17,25},{25,17},{2,10},{10... | collective-permute-start | bytes 98312 | tf_op jit(solution)/shard_map/ppermute | solution.py:328
  44.3 2.8 %collective-permute-start.11 = (f32[2,4,1024]{2,1,0:T(4,128)S(1)}, f32[2,4,1024]{2,1,0:T(4,128)S(1)}, u32[]{:S(2)}, u32[]{:S(2)}) collective-permute-start(f32[2,4,1024]{2,1,0:T(4,128)S(1)} %get-tuple-element.27), channel_id=1, source_target_pairs={{0,16},{8,24},{16,0},{24,8},{1,17},{9,25},{17,1},{25,9},{2,18},{10... | collective-permute-start | bytes 98312 | tf_op jit(solution)/shard_map/ppermute | solution.py:328
  45.5 3.4 %collective-permute-start.12 = (f32[2,4,1024]{2,1,0:T(4,128)S(1)}, f32[2,4,1024]{2,1,0:T(4,128)S(1)}, u32[]{:S(2)}, u32[]{:S(2)}) collective-permute-start(f32[2,4,1024]{2,1,0:T(4,128)S(1)} %get-tuple-element.28), channel_id=1, source_target_pairs={{0,24},{8,16},{16,8},{24,0},{1,25},{9,17},{17,9},{25,1},{2,26},{10... | collective-permute-start | bytes 98312 | tf_op jit(solution)/shard_map/ppermute | solution.py:328
